TPU v7x, 768 devices: a whole 4x8x12 slice. The times are simulated.
768 devices in a mesh: ctx: 48 (over y_hi, z), head: 16 (over x, y_lo, core).
Axes of the slice: x: 4, y: 8 (y_hi: 4, y_lo: 2; y = y_hi * 2 + y_lo), z: 12, core: 2. Of those that a mesh axis runs over, the one named last changes fastest.
Arguments:
- queries: bfloat16 [6144, 8192], P('ctx', 'head'), may hold values from -224 to 224
- key_rows: bfloat16 [6144, 1024], P('ctx'), may hold values from -16 to 16
- value_rows: bfloat16 [6144, 1024], P('ctx'), may hold values from -6 to 6
- block_flags: int32 [96, 96], P('ctx'), may hold values from 0 to 1, as said below
- out_weight: bfloat16 [8192, 8192], P('head'), may hold values from -0.125 to 0.125
Outputs:
- projected: bfloat16 [6144, 8192], P(('ctx', 'head'))
Inputs may be any that keep to these rules, and one draw needn't show every extreme that they name: `block_flags`: 0 or 1; zero above the diagonal, one on it.
All inputs are finite; a program needn't handle non-finite values.
Results may differ from a plain program's by a relative error of at most 0.0085.
Values may be sent and summed in bfloat16 or wider, within the bound.
A program may use at most 32 MiB of HBM per device.

v0:
```python
import math

import jax
import jax.numpy as jnp
from jax import lax
from jax.sharding import PartitionSpec as P

QH = 64
KVH = 8
HD = 128
BLOCK = 64


def local(queries, key_rows, value_rows, block_flags, out_weight):
    tok_rows = queries.shape[0]
    local_heads = queries.shape[1] // HD
    group = QH // KVH
    kv_local = max(1, local_heads // group)
    sub_heads = local_heads // kv_local
    scale_factor = 1.0 / math.sqrt(HD)
    first_kv = lax.axis_index("head") * local_heads // group
    key_own = lax.dynamic_slice_in_dim(key_rows, first_kv * HD, kv_local * HD, 1)
    value_own = lax.dynamic_slice_in_dim(value_rows, first_kv * HD, kv_local * HD, 1)
    own_index = lax.axis_index("ctx")
    row_start = own_index * tok_rows
    rows = queries.shape[0]
    positions = row_start + jnp.arange(rows, dtype=jnp.int32)
    query_sets = [
        (
            queries.reshape(rows, kv_local, sub_heads, HD),
            positions,
            block_flags,
            row_start + rows - 1,
        )
    ]

    def attend_block(state, query_set, key_block, value_block, start):
        query_tiles, query_pos, flag_rows, query_last = query_set
        width = key_block.shape[0]
        key_three = key_block.reshape(width, kv_local, HD)
        value_three = value_block.reshape(width, kv_local, HD)
        scores = (
            jnp.einsum("qkgd,rkd->kgqr", query_tiles, key_three, preferred_element_type=jnp.float32)
            * scale_factor
        )
        flag_part = lax.dynamic_slice_in_dim(flag_rows, start // BLOCK, width // BLOCK, 1)
        flag_full = jnp.repeat(jnp.repeat(flag_part, BLOCK, axis=0), BLOCK, axis=1) == 1
        key_pos = start + jnp.arange(width, dtype=jnp.int32)
        allowed = flag_full & (key_pos[None, :] <= query_pos[:, None])
        scores = jnp.where(allowed, scores, -1e30)
        run_max, run_sum, accum = state
        new_max = jnp.maximum(run_max, jnp.max(scores, axis=-1))
        weights = jnp.where(allowed, jnp.exp(scores - new_max[..., None]), 0.0)
        factor = jnp.exp(run_max - new_max)
        new_sum = run_sum * factor + jnp.sum(weights, axis=-1)
        update = jnp.einsum(
            "kgqr,rkd->kgqd",
            weights.astype(jnp.bfloat16),
            value_three,
            preferred_element_type=jnp.float32,
        )
        return (new_max, new_sum, accum * factor[..., None] + update)

    initial = tuple(
        (
            (
                jnp.full((kv_local, sub_heads, qs[0].shape[0]), -1e30, jnp.float32),
                jnp.zeros((kv_local, sub_heads, qs[0].shape[0]), jnp.float32),
                jnp.zeros((kv_local, sub_heads, qs[0].shape[0], HD), jnp.float32),
            )
            for qs in query_sets
        )
    )
    query_set = query_sets[0]
    state = initial[0]
    key_piece = lax.all_gather(key_own, "ctx", axis=0, tiled=True)
    value_piece = lax.all_gather(value_own, "ctx", axis=0, tiled=True)
    rows = key_piece.shape[0]
    width = BLOCK
    while width * 2 <= 512 and rows % (width * 2) == 0:
        width = width * 2

    def inner(index, inner_state):
        key_block = lax.dynamic_slice_in_dim(key_piece, index * width, width, 0)
        value_block = lax.dynamic_slice_in_dim(value_piece, index * width, width, 0)
        return attend_block(inner_state, query_set, key_block, value_block, index * width)

    state = lax.fori_loop(0, rows // width, inner, state)
    results = [state]
    final = tuple(results)
    run_max, run_sum, accum = final[0]
    normalized = accum / run_sum[..., None]
    rows = normalized.shape[2]
    attended = (
        jnp.transpose(normalized, (2, 0, 1, 3)).reshape(rows, local_heads * HD).astype(jnp.bfloat16)
    )
    summed = lax.psum_scatter(
        jnp.dot(attended, out_weight, preferred_element_type=jnp.float32),
        "head",
        scatter_dimension=0,
        tiled=True,
    )
    return summed.astype(jnp.bfloat16)


def solution(mesh):
    placed = (P("ctx", "head"), P("ctx", None), P("ctx", None), P("ctx", None), P("head", None))
    return jax.shard_map(
        local, mesh=mesh, in_specs=placed, out_specs=P(("ctx", "head"), None), check_vma=False
    )
```

profile of v0, /device:TPU:57, one launch (start us, length us, event | category | flops | bytes accessed | tf_op | source)
XLA Modules:
  0.0 383.0 jit_solution(15287416252865781402)
XLA Ops:
  6.5 0.9 copy-done
  7.5 0.6 constant_dynamic-slice_fusion.2
  8.2 1.4 constant_dynamic-slice_fusion.1
  9.7 1.0 copy.9
  10.9 117.6 %all-gather.3.cloned.1.call-done = bf16[6144,128]{1,0:T(8,128)(2,1)} async-done(((bf16[128,128]{1,0:T(8,128)(2,1)}), bf16[6144,128]{1,0:T(8,128)(2,1)}) %all-gather.3.cloned.1.call-update) | async-done | bytes 1572880 | tf_op jit(solution)/shard_map/all_gather | solution.py:76
  128.4 117.1 %all-gather.5.cloned.1.call-done = bf16[6144,128]{1,0:T(8,128)(2,1)} async-done(((bf16[128,128]{1,0:T(8,128)(2,1)}), bf16[6144,128]{1,0:T(8,128)(2,1)}) %all-gather.5.cloned.1.call-update) | async-done | bytes 1572880 | tf_op jit(solution)/shard_map/all_gather | solution.py:77
  245.5 48.7 %while.20 = (s32[]{:T(128)}, f32[1,4,128]{2,1,0:T(4,128)S(1)}, f32[1,4,128]{2,1,0:T(4,128)S(1)}, f32[1,4,128,128]{3,2,1,0:T(8,128)S(1)}, s32[2,96]{1,0:T(2,128)}...) while((s32[]{:T(128)}, f32[1,4,128]{2,1,0:T(4,128)S(1)}, ...), condition=%wide.region_3.4_spmd.clone, body=%wide.region_0.3_spmd.clone.sunk | while | flops 136908448 | bytes 4368122 | solution.py:88
  245.5 0.7 constant_dynamic-slice_fusion.4
  246.7 1.2 fusion.33
  247.9 1.4 fusion.36
  249.3 0.2 fusion.35
  249.5 0.8 constant_dynamic-slice_fusion.4
  250.7 1.2 fusion.33
  252.0 1.3 fusion.36
  253.6 0.8 constant_dynamic-slice_fusion.4
  254.8 1.2 fusion.33
  256.0 1.3 fusion.36
  257.4 0.2 fusion.35
  257.7 0.8 constant_dynamic-slice_fusion.4
  258.8 1.2 fusion.33
  260.1 1.3 fusion.36
  261.7 0.8 constant_dynamic-slice_fusion.4
  262.9 1.2 fusion.33
  264.1 1.3 fusion.36
  265.8 0.8 constant_dynamic-slice_fusion.4
  267.0 1.2 fusion.33
  268.2 1.3 fusion.36
  269.8 0.8 constant_dynamic-slice_fusion.4
  271.0 1.2 fusion.33
  272.3 1.3 fusion.36
  273.9 0.8 constant_dynamic-slice_fusion.4
  275.1 1.2 fusion.33
  276.3 1.3 fusion.36
  278.0 0.8 constant_dynamic-slice_fusion.4
  279.1 1.2 fusion.33
  280.4 1.3 fusion.36
  282.0 0.8 constant_dynamic-slice_fusion.4
  283.2 1.2 fusion.33
  284.4 1.3 fusion.36
  286.1 0.8 constant_dynamic-slice_fusion.4
  287.3 1.2 fusion.33
  288.5 1.3 fusion.36
  290.1 0.8 constant_dynamic-slice_fusion.4
  291.3 1.2 fusion.33
  292.6 1.3 fusion.36
  294.3 6.6 %fusion.22 = f32[128,8192]{1,0:T(8,128)} fusion(bf16[128,512]{0,1:T(8,128)(2,1)S(1)} %bitcast.65, bf16[512,8192]{1,0:T(8,128)(2,1)} %param.11), kind=kOutput, calls=%fused_computation.36 | convolution fusion | flops 1073741824 | bytes 12713984 | tf_op jit(solution)/shard_map/dot_general | solution.py:98
  301.0 73.8 %reduce-scatter.2.cloned.1.call-done = f32[8,8192]{1,0:T(8,128)} async-done(((f32[128,8192]{1,0:T(8,128)}), f32[8,8192]{1,0:T(8,128)}) %reduce-scatter.2.cloned.1.call-update) | async-done | bytes 262160 | tf_op jit(solution)/shard_map/reduce_scatter | solution.py:97
  374.8 1.6 convert_element_type.25
  (143 shorter events, 7.7 us)
Async XLA Ops:
  6.5 1.0 copy-start
  6.5 121.9 %all-gather.3.cloned.1.call-start = ((), (), s32[]{:S(2)}) async-start(), calls=%async_computation.1 | async-start | bytes 1605632 | tf_op jit(solution)/shard_map/all_gather | solution.py:76
  8.1 237.4 %all-gather.5.cloned.1.call-start = ((), (), s32[]{:S(2)}) async-start(), calls=%async_computation.2 | async-start | bytes 1605632 | tf_op jit(solution)/shard_map/all_gather | solution.py:77
  9.6 365.2 %reduce-scatter.2.cloned.1.call-start = ((), (), s32[]{:S(2)}) async-start(), calls=%async_computation.3 | async-start | bytes 4456448 | tf_op jit(solution)/shard_map/reduce_scatter | solution.py:97
Sparse Core Ops, SparseCore 0:
  10.9 117.4 all-gather.2
  132.0 113.4 all-gather.4
  301.1 73.6 reduce-scatter.1
where the time goes:
time: 390 us; the launch traced here: 383 us
  waiting for transfers between devices  309 us (79%)
  matrix products  37.5 us (10%)
  local copies, waits for them, and re-layouts  16.3 us (4%)
  between operations  13.2 us (3%)
  other arithmetic  6.31 us (2%)
    all_gather x1, waiting for transfers between devices, local(): key_piece = lax.all_gather(key_own, 'ctx', axis=0, tiled=True)  118 us
    all_gather x1, waiting for transfers between devices, local(): value_piece = lax.all_gather(value_own, 'ctx', axis=0, tiled=True)  117 us
    reduce_scatter x1, waiting for transfers between devices, local(): lax.psum_scatter(jnp.dot(attended, out_weight, preferred_element_type=jnp...  73.8 us
    dot_general x12, matrix products, attend_block(): jnp.einsum('kgqr,rkd->kgqd', weights.astype(jnp.bfloat16), value_three, p...  16.2 us
    dot_general x12, matrix products, attend_block(): jnp.einsum('qkgd,rkd->kgqr', query_tiles, key_three, preferred_element_ty...  14.6 us
    dynamic_slice x24, local copies, waits for them, and re-layouts, attend_block(): lax.dynamic_slice_in_dim(flag_rows, start // BLOCK, width // BLOCK, 1)  10.1 us
  transfers between devices with their start and end apart: 3, of which 3 were waited for; matrix products, arithmetic and copies ran while one was open for 1% of the time, Pallas kernels for 0%

commit v1 on v0

v1 whole, which is shorter than its diff:
```python
import math

import jax
import jax.numpy as jnp
from jax import lax
from jax.experimental import pallas as pl
from jax.experimental.pallas import tpu as pltpu
from jax.sharding import PartitionSpec as P

MESH = pl.DeviceIdType.MESH
HD = 128
TOK = 128
HALF = 64
NZ = 12
NX = 4
NR = 4
COLS = 4096
CW = 512
NC = COLS // CW
SCALE = math.log2(math.e) / math.sqrt(HD)
NEG = 1e30
FLOOR = -1e20
F32 = jnp.float32
BF16 = jnp.bfloat16


def kernel(
    q_ref, k_ref, v_ref, flags, w_ref, out_ref,
    kv, oth, qall, qt, vt, acc, racc, a2, wv, sbuf, own, r1, r1x, s2a, s2b, s2d, f0, f1, own2,
    lsem, wsem, ytx, yrx, tx, rx, qsem, wrem, atx, arx, t1, q1, t2, q2, t3, q3,
):
    c = lax.axis_index("ctx")
    h = lax.axis_index("head")
    r, z = lax.div(c, NZ), lax.rem(c, NZ)
    x, yl, co = lax.div(h, 4), lax.rem(lax.div(h, 2), 2), lax.rem(h, 2)
    sg = 1 - 2 * yl

    def dev(rr, zz, xx, yy, cc):
        return {"ctx": rr * NZ + zz, "head": xx * 4 + yy * 2 + cc}

    zp = dev(r, lax.rem(z + 1, NZ), x, yl, co)
    zm = dev(r, lax.rem(z + NZ - 1, NZ), x, yl, co)
    r_minus, r_plus, r_far = lax.rem(r - sg + NR, NR), lax.rem(r + sg + NR, NR), lax.rem(r + 2, NR)
    dev_a = dev(r_minus, z, x, 1 - yl, co)
    dev_b = dev(r_minus, z, x, yl, co)
    dev_b_src = dev(r_plus, z, x, yl, co)
    dev_c = dev(r_far, z, x, 1 - yl, co)
    mate = dev(r, z, x, yl, 1 - co)

    def xdev(d, cc):
        return dev(r, z, lax.rem(x + d, NX), yl, cc)

    def ydev(cc):
        return dev(r, z, x, 1 - yl, cc)

    row_of = (r, r_minus, r_plus, r_far)

    head_own = x * 2 + yl
    head_oth = x * 2 + 1 - yl
    rows = pl.ds(pl.multiple_of(co * HALF, HALF), HALF)

    def head_cols(kvh):
        return pl.ds(pl.multiple_of(kvh * HD, HD), HD)

    loads = [
        pltpu.make_async_copy(k_ref.at[rows, head_cols(head_own)], kv.at[z, 0, :, pl.ds(0, HD)], lsem.at[0]),
        pltpu.make_async_copy(v_ref.at[rows, head_cols(head_own)], kv.at[z, 0, :, pl.ds(HD, HD)], lsem.at[1]),
        pltpu.make_async_copy(k_ref.at[rows, head_cols(head_oth)], oth.at[:, pl.ds(0, HD)], lsem.at[2]),
        pltpu.make_async_copy(v_ref.at[rows, head_cols(head_oth)], oth.at[:, pl.ds(HD, HD)], lsem.at[3]),
        pltpu.make_async_copy(q_ref, qall.at[co], lsem.at[4]),
    ]
    for copy in loads:
        copy.start()
    w_own = pltpu.make_async_copy(
        w_ref.at[:, pl.ds(pl.multiple_of(co * COLS, COLS), COLS)], wv.at[co], wsem
    )
    w_own.start()

    barrier = pltpu.get_barrier_semaphore()
    peers = [zp, zm, dev_a, dev_b_src, dev_c, mate, ydev(0), ydev(1)]
    peers += [xdev(d, cc) for d in (1, 2, 3) for cc in (0, 1)]
    for peer in peers:
        pl.semaphore_signal(barrier, inc=1, device_id=peer, device_id_type=MESH)
    pl.semaphore_wait(barrier, len(peers))

    def remote(src, dst, send_sem, recv_sem, peer):
        return pltpu.make_async_remote_copy(
            src_ref=src, dst_ref=dst, send_sem=send_sem, recv_sem=recv_sem, device_id=peer, device_id_type=MESH
        )

    def at_plus(d):
        return lax.rem(z + NZ - d, NZ)

    def at_minus(d):
        return lax.rem(z + d, NZ)

    def hop(way, d, j):
        zi = at_plus(d) if way == 0 else at_minus(d)
        return remote(kv.at[zi, j], kv.at[zi, j], tx.at[way, d, j], rx.at[way, d, j], zp if way == 0 else zm)

    def arrival(way, d, j):
        zi = at_plus(d) if way == 0 else at_minus(d)
        return remote(kv.at[zi, j], kv.at[zi, j], tx.at[way, d - 1, j], rx.at[way, d - 1, j], zp if way == 0 else zm)

    for copy in loads[:2]:
        copy.wait()
    hop(0, 0, 0).start()
    hop(1, 0, 0).start()
    for copy in loads[2:4]:
        copy.wait()
    y_copies = [
        remote(oth, kv.at[z, 1], ytx.at[0], yrx.at[0], dev_a),
        remote(kv.at[z, 0], kv.at[z, 2], ytx.at[1], yrx.at[1], dev_b),
        remote(oth, kv.at[z, 3], ytx.at[2], yrx.at[2], dev_c),
    ]
    for copy in y_copies:
        copy.start()
    q_copy = remote(q_ref, qall.at[co], qsem.at[0], qsem.at[1], mate)
    q_copy.start()
    w_copy = remote(
        w_ref.at[:, pl.ds(pl.multiple_of((1 - co) * COLS, COLS), COLS)], wv.at[co], wrem.at[0], wrem.at[1], mate
    )
    w_copy.start()

    lane = lax.broadcasted_iota(jnp.int32, (1, 2 * TOK), 1)
    first_half = lax.rem(lane, TOK) < HALF

    loads[4].wait()
    q_copy.wait_recv()
    for i in range(8):
        qt[i] = qall[i // 4, :, (i % 4) * HD : (i % 4 + 1) * HD].T
    for g in range(4):
        acc[g, :HD] = jnp.zeros((HD, 2 * TOK), F32)
        acc[g, HD : HD + 8] = jnp.where(
            lax.broadcasted_iota(jnp.int32, (8, 2 * TOK), 0) == 0, FLOOR, 0.0
        )

    for j in (1, 2, 3):
        y_copies[j - 1].wait_recv()
        hop(0, 0, j).start()
        hop(1, 0, j).start()

    def prepare(slot, zi):
        vt[slot] = kv[zi, :, :, HD:].reshape(4 * HALF, HD).T

    def item(slot, zi, g, diagonal=False):
        keys = kv[zi, :, :, :HD].reshape(4 * HALF, HD)
        query = jnp.concatenate([qt[2 * g], qt[2 * g + 1]], axis=1)
        scores = jnp.dot(keys, query, preferred_element_type=F32)
        parts = []
        for j in range(4):
            at = 2 * (row_of[j] * NZ + zi) + co
            flag = jnp.where(first_half, flags[0, at], flags[1, at]).astype(F32)
            bias = (flag - 1.0) * NEG
            if diagonal and j == 0:
                key_pos = co * HALF + lax.broadcasted_iota(jnp.int32, (HALF, 2 * TOK), 0)
                query_pos = lax.rem(lax.broadcasted_iota(jnp.int32, (HALF, 2 * TOK), 1), TOK)
                bias = jnp.where(key_pos <= query_pos, bias, -NEG)
            parts.append(scores[j * HALF : (j + 1) * HALF] * SCALE + bias)
        scores = jnp.concatenate(parts, axis=0)
        old = acc[g, HD : HD + 1]
        new = jnp.maximum(old, jnp.max(scores, axis=0, keepdims=True))
        weights = jnp.exp2(scores - new)
        factor = jnp.exp2(old - new)
        acc[g, HD : HD + 1] = new
        acc[g, HD + 1 : HD + 2] = acc[g, HD + 1 : HD + 2] * factor + jnp.sum(weights, axis=0, keepdims=True)
        acc[g, :HD] = acc[g, :HD] * factor + jnp.dot(vt[slot], weights.astype(BF16), preferred_element_type=F32)

    for j in range(4):
        arrival(0, 1, j).wait_recv()
        hop(0, 1, j).start()
        arrival(1, 1, j).wait_recv()
        hop(1, 1, j).start()
        if j == 0:
            prepare(0, z)
        item(0, z, j, diagonal=True)

    def step(d, carry):
        for j in range(4):
            for way in (0, 1):
                late = (j < 2) == (way == 0)
                if late:
                    arrival(way, d, j).wait_recv()

                    @pl.when(d < 6)
                    def _():
                        hop(way, d, j).start()
                else:

                    @pl.when(d < 6)
                    def _():
                        arrival(way, d, j).wait_recv()

                    @pl.when(d < 5)
                    def _():
                        hop(way, d, j).start()

            if j == 0:
                prepare(0, at_plus(d - 1))
                prepare(1, at_minus(d - 1))
            item(0, at_plus(d - 1), j)
            item(1, at_minus(d - 1), j)
        return carry

    lax.fori_loop(2, 7, step, 0)

    a_copies = [remote(acc.at[g], racc.at[g], atx.at[g], arx.at[g], mate) for g in range(4)]
    prepare(0, at_minus(6))
    for g in range(4):
        item(0, at_minus(6), g)
        a_copies[g].start()

    def place(xx, yy):
        dx = lax.rem(xx - x + NX + 3, NX)
        near = lax.rem(yy + yl, 2)
        by_y = dx + 4 * (1 - near)
        by_x = dx * 2 + near
        return jnp.where(co == 0, by_y, by_x)

    for g in range(4):
        a_copies[g].wait_recv()
        m0, m1 = acc[g, HD : HD + 1], racc[g, HD : HD + 1]
        top = jnp.maximum(m0, m1)
        e0, e1 = jnp.exp2(m0 - top), jnp.exp2(m1 - top)
        total = acc[g, HD + 1 : HD + 2] * e0 + racc[g, HD + 1 : HD + 2] * e1
        mixed = (acc[g, :HD] * e0 + racc[g, :HD] * e1) / total
        for i in (0, 1):
            tile = mixed[:, i * TOK : (i + 1) * TOK].T.astype(BF16)
            cols = slice((2 * g + i) * HD, (2 * g + i + 1) * HD)
            for xx in range(4):
                for yy in range(2):
                    at = (xx * 2 + yy) * 16
                    a2[place(xx, yy), :, cols] = tile[at : at + 16]

    w_own.wait()
    w_copy.wait_recv()

    def send1y(n):
        return remote(sbuf.at[n, pl.ds(0, 64)], r1.at[n], t1.at[0, n], q1.at[0, n], ydev(0))

    def send1x(n, d):
        return remote(
            sbuf.at[n, pl.ds(32 * (d - 1), 32)], r1x.at[d - 1, n], t1.at[d - 1, n], q1.at[d - 1, n], xdev(d, 1)
        )

    def project(n, carry):
        cols = pl.ds(pl.multiple_of(n * CW, CW), CW)
        part = jnp.dot(
            a2[...].reshape(TOK, 8 * HD), wv[:, :, cols].reshape(8 * HD, CW), preferred_element_type=F32
        )
        sbuf[n] = part[:96].astype(BF16)
        own[n] = part[64:]

        @pl.when(co == 0)
        def _():
            send1y(n).start()

        @pl.when(co == 1)
        def _():
            for d in (2, 1, 3):
                send1x(n, d).start()

        return carry

    lax.fori_loop(0, NC, project, 0)

    def send2x(n, d, cc):
        return remote(s2a.at[n, d - 1, cc], f0.at[d - 1, n], t2.at[d - 1, cc, n], q2.at[d - 1, n], xdev(d, cc))

    def send2y(n, cc):
        return remote(s2b.at[n, cc], f1.at[0, n], t2.at[0, cc, n], q2.at[3, n], ydev(cc))

    def send3a(n):
        return remote(s2d.at[n], f0.at[3, n], t3.at[n], q3.at[n], mate)

    def send3b(n):
        return remote(s2d.at[n], f1.at[1, n], t3.at[n], q3.at[n], mate)

    @pl.when(co == 0)
    def _():
        def second(n, carry):
            send1y(n).wait_recv()
            total = own[n] + r1[n].astype(F32)
            for d in (2, 1, 3):
                for cc in (0, 1):
                    at = 16 * (d - 1) + 8 * cc
                    s2a[n, d - 1, cc] = total[at : at + 8].astype(BF16)
                    send2x(n, d, cc).start()
            own2[n] = total[48:56]
            s2d[n] = total[56:].astype(BF16)
            send3a(n).start()
            return carry

        lax.fori_loop(0, NC, second, 0)

        def last(n, carry):
            for d in (1, 2, 3):
                send2x(n, d, 0).wait_recv()
            total = own2[n] + f0[0, n].astype(F32) + f0[1, n].astype(F32) + f0[2, n].astype(F32)
            out_ref[:, pl.ds(pl.multiple_of(n * CW, CW), CW)] = total.astype(BF16)
            send2y(n, 0).wait_recv()
            send3b(n).wait_recv()
            total = f1[0, n].astype(F32) + f1[1, n].astype(F32)
            out_ref[:, pl.ds(pl.multiple_of(COLS + n * CW, CW), CW)] = total.astype(BF16)
            return carry

        lax.fori_loop(0, NC, last, 0)

        def sent(n, carry):
            send1y(n).wait_send()
            for d in (1, 2, 3):
                for cc in (0, 1):
                    send2x(n, d, cc).wait_send()
            send3a(n).wait_send()
            return carry

        lax.fori_loop(0, NC, sent, 0)

    @pl.when(co == 1)
    def _():
        def second(n, carry):
            for d in (1, 2, 3):
                send1x(n, d).wait_recv()
            total = own[n, pl.ds(32, 32)]
            for d in range(3):
                total = total + r1x[d, n].astype(F32)
            for cc in (0, 1):
                s2b[n, cc] = total[16 + 8 * cc : 24 + 8 * cc].astype(BF16)
                send2y(n, cc).start()
            s2d[n] = total[:8].astype(BF16)
            send3b(n).start()
            own2[n] = total[8:16]
            return carry

        lax.fori_loop(0, NC, second, 0)

        def last(n, carry):
            for d in (1, 2, 3):
                send2x(n, d, 1).wait_recv()
            send3a(n).wait_recv()
            total = f0[3, n].astype(F32) + f0[0, n].astype(F32) + f0[1, n].astype(F32) + f0[2, n].astype(F32)
            out_ref[:, pl.ds(pl.multiple_of(n * CW, CW), CW)] = total.astype(BF16)
            send2y(n, 1).wait_recv()
            total = own2[n] + f1[0, n].astype(F32)
            out_ref[:, pl.ds(pl.multiple_of(COLS + n * CW, CW), CW)] = total.astype(BF16)
            return carry

        lax.fori_loop(0, NC, last, 0)

        def sent(n, carry):
            for d in (1, 2, 3):
                send1x(n, d).wait_send()
            for cc in (0, 1):
                send2y(n, cc).wait_send()
            send3b(n).wait_send()
            return carry

        lax.fori_loop(0, NC, sent, 0)

    for copy in y_copies + [q_copy, w_copy] + a_copies:
        copy.wait_send()

    def drain(d, carry):
        for j in range(4):
            for way in (0, 1):
                if (j < 2) == (way == 0):
                    hop(way, d, j).wait_send()
                else:

                    @pl.when(d < 5)
                    def _():
                        hop(way, d, j).wait_send()

        return carry

    lax.fori_loop(0, 6, drain, 0)


def local(queries, key_rows, value_rows, block_flags, out_weight):
    dma = pltpu.SemaphoreType.DMA
    hbm = pl.BlockSpec(memory_space=pl.ANY)
    vmem = pltpu.VMEM
    return pl.pallas_call(
        kernel,
        out_shape=jax.ShapeDtypeStruct((8, 2 * COLS), BF16),
        in_specs=[hbm, hbm, hbm, pl.BlockSpec(memory_space=pltpu.SMEM), hbm],
        out_specs=pl.BlockSpec(memory_space=pltpu.VMEM),
        scratch_shapes=[
            vmem((NZ, 4, HALF, 2 * HD), BF16),
            vmem((HALF, 2 * HD), BF16),
            vmem((2, TOK, 4 * HD), BF16),
            vmem((8, HD, TOK), BF16),
            vmem((2, HD, 4 * HALF), BF16),
            vmem((4, HD + 8, 2 * TOK), F32),
            vmem((4, HD + 8, 2 * TOK), F32),
            vmem((8, 16, 8 * HD), BF16),
            vmem((2, 4 * HD, COLS), BF16),
            vmem((NC, 96, CW), BF16),
            vmem((NC, 64, CW), F32),
            vmem((NC, 64, CW), BF16),
            vmem((3, NC, 32, CW), BF16),
            vmem((NC, 3, 2, 8, CW), BF16),
            vmem((NC, 2, 8, CW), BF16),
            vmem((NC, 8, CW), BF16),
            vmem((4, NC, 8, CW), BF16),
            vmem((2, NC, 8, CW), BF16),
            vmem((NC, 8, CW), F32),
            dma((5,)),
            dma,
            dma((3,)),
            dma((3,)),
            dma((2, 6, 4)),
            dma((2, 6, 4)),
            dma((2,)),
            dma((2,)),
            dma((4,)),
            dma((4,)),
            dma((3, NC)),
            dma((3, NC)),
            dma((3, 2, NC)),
            dma((4, NC)),
            dma((NC,)),
            dma((NC,)),
        ],
        compiler_params=pltpu.CompilerParams(
            collective_id=0, has_side_effects=True, vmem_limit_bytes=60 * 2**20
        ),
        name="attention_layer",
    )(queries, key_rows, value_rows, block_flags, out_weight)


def solution(mesh):
    placed = (P("ctx", "head"), P("ctx", None), P("ctx", None), P("ctx", None), P("head", None))
    return jax.shard_map(
        local, mesh=mesh, in_specs=placed, out_specs=P(("ctx", "head"), None), check_vma=False
    )
```

time: 390 us -> 67.7 us (0.17)
  the two profiles are of different devices: /device:TPU:57 before, /device:TPU:1 now
where the time goes in v1:
time: 67.7 us; the launch traced here: 67.5 us
  Pallas kernels  65.9 us (97%)
  local copies, waits for them, and re-layouts  1.57 us (2%)
    pallas_call x1, Pallas kernels, local(): pl.pallas_call(kernel, out_shape=jax.ShapeDtypeStruct((8, 2 * COLS), BF16...  65.9 us
    unnamed x1, local copies, waits for them, and re-layouts  1.57 us

profile of v1, /device:TPU:1, one launch (start us, length us, event | category | flops | bytes accessed | tf_op | source)
XLA Modules:
  0.0 67.5 jit_solution(1873781505394003424)
XLA Ops:
  0.0 65.9 %attention_layer.1 = bf16[8,8192]{1,0:T(8,128)(2,1)} custom-call(bf16[128,512]{1,0:T(8,128)(2,1)} %q_ref.1, bf16[128,1024]{1,0:T(8,128)(2,1)} %k_ref.1, bf16[128,1024]{1,0:T(8,128)(2,1)} %v_ref.1, s32[2,96]{1,0:T(2,128)} %flags.1, bf16[512,8192]{1,0:T(8,128)(2,1)} %w_ref.1), custom_call_target="tpu_custom_call" | custom-call | tf_op jit(solution)/shard_map/attention_layer/pallas_call | solution.py:383
  65.9 1.6 %copy.7 = bf16[8,8192]{1,0:T(8,128)(2,1)} copy(bf16[8,8192]{1,0:T(8,128)(2,1)} %attention_layer.1) | data formatting | bytes 262144

commit v2 on v1

--- a/solution.py
+++ b/solution.py
@@ -25,9 +25,9 @@
 
 
 def kernel(
-    q_ref, k_ref, v_ref, flags, w_ref, out_ref,
-    kv, oth, qall, qt, vt, acc, racc, a2, wv, sbuf, own, r1, r1x, s2a, s2b, s2d, f0, f1, own2,
-    lsem, wsem, ytx, yrx, tx, rx, qsem, wrem, atx, arx, t1, q1, t2, q2, t3, q3,
+    q_ref, k_ref, v_ref, flags_ref, w_ref, out_ref,
+    flags, obuf, kv, oth, qall, qt, vt, acc, racc, a2, wv, sbuf, own, r1, r1x, s2a, s2b, s2d, f0, f1, own2,
+    lsem, wsem, fsem, osem, ytx, yrx, tx, rx, qsem, wrem, atx, arx, t1, q1, t2, q2, t3, q3,
 ):
     c = lax.axis_index("ctx")
     h = lax.axis_index("head")
@@ -71,6 +71,8 @@
     ]
     for copy in loads:
         copy.start()
+    flag_load = pltpu.make_async_copy(flags_ref, flags, fsem)
+    flag_load.start()
     w_own = pltpu.make_async_copy(
         w_ref.at[:, pl.ds(pl.multiple_of(co * COLS, COLS), COLS)], wv.at[co], wsem
     )
@@ -113,7 +115,7 @@
         remote(kv.at[z, 0], kv.at[z, 2], ytx.at[1], yrx.at[1], dev_b),
         remote(oth, kv.at[z, 3], ytx.at[2], yrx.at[2], dev_c),
     ]
-    for copy in y_copies:
+    for copy in reversed(y_copies):
         copy.start()
     q_copy = remote(q_ref, qall.at[co], qsem.at[0], qsem.at[1], mate)
     q_copy.start()
@@ -128,78 +130,91 @@
     loads[4].wait()
     q_copy.wait_recv()
     for i in range(8):
-        qt[i] = qall[i // 4, :, (i % 4) * HD : (i % 4 + 1) * HD].T
+        side = slice((i % 2) * TOK, (i % 2 + 1) * TOK)
+        qt[i // 2, :, side] = qall[i // 4, :, (i % 4) * HD : (i % 4 + 1) * HD].T
     for g in range(4):
         acc[g, :HD] = jnp.zeros((HD, 2 * TOK), F32)
         acc[g, HD : HD + 8] = jnp.where(
             lax.broadcasted_iota(jnp.int32, (8, 2 * TOK), 0) == 0, FLOOR, 0.0
         )
 
+    def relay(way, d, j):
+        last = 6 if (j < 2) == (way == 0) else 5
+
+        def go():
+            arrival(way, d, j).wait_recv()
+
+        def on():
+            hop(way, d, j).start()
+
+        if isinstance(d, int):
+            if d <= last:
+                go()
+            if d < last:
+                on()
+        else:
+            pl.when(d <= last)(go)
+            pl.when(d < last)(on)
+
+    for way in (0, 1):
+        relay(way, 1, 0)
     for j in (1, 2, 3):
         y_copies[j - 1].wait_recv()
         hop(0, 0, j).start()
         hop(1, 0, j).start()
-
+    flag_load.wait()
     def prepare(slot, zi):
         vt[slot] = kv[zi, :, :, HD:].reshape(4 * HALF, HD).T
 
-    def item(slot, zi, g, diagonal=False):
-        keys = kv[zi, :, :, :HD].reshape(4 * HALF, HD)
-        query = jnp.concatenate([qt[2 * g], qt[2 * g + 1]], axis=1)
-        scores = jnp.dot(keys, query, preferred_element_type=F32)
-        parts = []
-        for j in range(4):
-            at = 2 * (row_of[j] * NZ + zi) + co
-            flag = jnp.where(first_half, flags[0, at], flags[1, at]).astype(F32)
-            bias = (flag - 1.0) * NEG
-            if diagonal and j == 0:
-                key_pos = co * HALF + lax.broadcasted_iota(jnp.int32, (HALF, 2 * TOK), 0)
-                query_pos = lax.rem(lax.broadcasted_iota(jnp.int32, (HALF, 2 * TOK), 1), TOK)
-                bias = jnp.where(key_pos <= query_pos, bias, -NEG)
-            parts.append(scores[j * HALF : (j + 1) * HALF] * SCALE + bias)
-        scores = jnp.concatenate(parts, axis=0)
+    def attend(bundles, g, diagonal=False):
+        query = qt[g]
         old = acc[g, HD : HD + 1]
-        new = jnp.maximum(old, jnp.max(scores, axis=0, keepdims=True))
-        weights = jnp.exp2(scores - new)
+        new = old
+        tiles = []
+        for slot, zi in bundles:
+            keys = kv[zi, :, :, :HD].reshape(4 * HALF, HD)
+            scores = jnp.dot(keys, query, preferred_element_type=F32)
+            parts = []
+            for j in range(4):
+                at = 2 * (row_of[j] * NZ + zi) + co
+                flag = jnp.where(first_half, flags[0, at], flags[1, at]).astype(F32)
+                bias = (flag - 1.0) * NEG
+                if diagonal and j == 0:
+                    key_pos = co * HALF + lax.broadcasted_iota(jnp.int32, (HALF, 2 * TOK), 0)
+                    query_pos = lax.rem(lax.broadcasted_iota(jnp.int32, (HALF, 2 * TOK), 1), TOK)
+                    bias = jnp.where(key_pos <= query_pos, bias, -NEG)
+                parts.append(scores[j * HALF : (j + 1) * HALF] * SCALE + bias)
+            scores = jnp.concatenate(parts, axis=0)
+            new = jnp.maximum(new, jnp.max(scores, axis=0, keepdims=True))
+            tiles.append(scores)
         factor = jnp.exp2(old - new)
+        total = acc[g, HD + 1 : HD + 2] * factor
+        mixed = acc[g, :HD] * factor
+        for (slot, _), scores in zip(bundles, tiles):
+            weights = jnp.exp2(scores - new)
+            total = total + jnp.sum(weights, axis=0, keepdims=True)
+            mixed = mixed + jnp.dot(vt[slot], weights.astype(BF16), preferred_element_type=F32)
         acc[g, HD : HD + 1] = new
-        acc[g, HD + 1 : HD + 2] = acc[g, HD + 1 : HD + 2] * factor + jnp.sum(weights, axis=0, keepdims=True)
-        acc[g, :HD] = acc[g, :HD] * factor + jnp.dot(vt[slot], weights.astype(BF16), preferred_element_type=F32)
+        acc[g, HD + 1 : HD + 2] = total
+        acc[g, :HD] = mixed
+
+    def relays(k, j):
+        for way in (0, 1):
+            relay(way, k + 1 if j == 0 else k, j)
 
     for j in range(4):
-        arrival(0, 1, j).wait_recv()
-        hop(0, 1, j).start()
-        arrival(1, 1, j).wait_recv()
-        hop(1, 1, j).start()
+        relays(1, j)
         if j == 0:
             prepare(0, z)
-        item(0, z, j, diagonal=True)
-
-    def step(d, carry):
+        attend([(0, z)], j, diagonal=True)
+
+    def step(k, carry):
         for j in range(4):
-            for way in (0, 1):
-                late = (j < 2) == (way == 0)
-                if late:
-                    arrival(way, d, j).wait_recv()
-
-                    @pl.when(d < 6)
-                    def _():
-                        hop(way, d, j).start()
-                else:
-
-                    @pl.when(d < 6)
-                    def _():
-                        arrival(way, d, j).wait_recv()
-
-                    @pl.when(d < 5)
-                    def _():
-                        hop(way, d, j).start()
-
+            relays(k, j)
             if j == 0:
-                prepare(0, at_plus(d - 1))
-                prepare(1, at_minus(d - 1))
-            item(0, at_plus(d - 1), j)
-            item(1, at_minus(d - 1), j)
+                prepare(0, at_plus(k - 1))
+                prepare(1, at_minus(k - 1))
+            attend([(0, at_plus(k - 1)), (1, at_minus(k - 1))], j)
         return carry
 
     lax.fori_loop(2, 7, step, 0)
@@ -207,7 +222,7 @@
     a_copies = [remote(acc.at[g], racc.at[g], atx.at[g], arx.at[g], mate) for g in range(4)]
     prepare(0, at_minus(6))
     for g in range(4):
-        item(0, at_minus(6), g)
+        attend([(0, at_minus(6))], g)
         a_copies[g].start()
 
     def place(xx, yy):
@@ -270,6 +285,10 @@
     def send2y(n, cc):
         return remote(s2b.at[n, cc], f1.at[0, n], t2.at[0, cc, n], q2.at[3, n], ydev(cc))
 
+    def put(side, n):
+        at = pl.multiple_of(side * COLS + n * CW, CW)
+        return pltpu.make_async_copy(obuf.at[side, n], out_ref.at[:, pl.ds(at, CW)], osem.at[side, n])
+
     def send3a(n):
         return remote(s2d.at[n], f0.at[3, n], t3.at[n], q3.at[n], mate)
 
@@ -297,11 +316,13 @@
             for d in (1, 2, 3):
                 send2x(n, d, 0).wait_recv()
             total = own2[n] + f0[0, n].astype(F32) + f0[1, n].astype(F32) + f0[2, n].astype(F32)
-            out_ref[:, pl.ds(pl.multiple_of(n * CW, CW), CW)] = total.astype(BF16)
+            obuf[0, n] = total.astype(BF16)
+            put(0, n).start()
             send2y(n, 0).wait_recv()
             send3b(n).wait_recv()
             total = f1[0, n].astype(F32) + f1[1, n].astype(F32)
-            out_ref[:, pl.ds(pl.multiple_of(COLS + n * CW, CW), CW)] = total.astype(BF16)
+            obuf[1, n] = total.astype(BF16)
+            put(1, n).start()
             return carry
 
         lax.fori_loop(0, NC, last, 0)
@@ -339,10 +360,12 @@
                 send2x(n, d, 1).wait_recv()
             send3a(n).wait_recv()
             total = f0[3, n].astype(F32) + f0[0, n].astype(F32) + f0[1, n].astype(F32) + f0[2, n].astype(F32)
-            out_ref[:, pl.ds(pl.multiple_of(n * CW, CW), CW)] = total.astype(BF16)
+            obuf[0, n] = total.astype(BF16)
+            put(0, n).start()
             send2y(n, 1).wait_recv()
             total = own2[n] + f1[0, n].astype(F32)
-            out_ref[:, pl.ds(pl.multiple_of(COLS + n * CW, CW), CW)] = total.astype(BF16)
+            obuf[1, n] = total.astype(BF16)
+            put(1, n).start()
             return carry
 
         lax.fori_loop(0, NC, last, 0)
@@ -356,6 +379,13 @@
             return carry
 
         lax.fori_loop(0, NC, sent, 0)
+
+    def stored(n, carry):
+        for side in (0, 1):
+            put(side, n).wait()
+        return carry
+
+    lax.fori_loop(0, NC, stored, 0)
 
     for copy in y_copies + [q_copy, w_copy] + a_copies:
         copy.wait_send()
@@ -383,13 +413,15 @@
     return pl.pallas_call(
         kernel,
         out_shape=jax.ShapeDtypeStruct((8, 2 * COLS), BF16),
-        in_specs=[hbm, hbm, hbm, pl.BlockSpec(memory_space=pltpu.SMEM), hbm],
-        out_specs=pl.BlockSpec(memory_space=pltpu.VMEM),
+        in_specs=[hbm] * 5,
+        out_specs=hbm,
         scratch_shapes=[
+            pltpu.SMEM((2, 96), jnp.int32),
+            vmem((2, NC, 8, CW), BF16),
             vmem((NZ, 4, HALF, 2 * HD), BF16),
             vmem((HALF, 2 * HD), BF16),
             vmem((2, TOK, 4 * HD), BF16),
-            vmem((8, HD, TOK), BF16),
+            vmem((4, HD, 2 * TOK), BF16),
             vmem((2, HD, 4 * HALF), BF16),
             vmem((4, HD + 8, 2 * TOK), F32),
             vmem((4, HD + 8, 2 * TOK), F32),
@@ -407,6 +439,8 @@
             vmem((NC, 8, CW), F32),
             dma((5,)),
             dma,
+            dma,
+            dma((2, NC)),
             dma((3,)),
             dma((3,)),
             dma((2, 6, 4)),

time: 67.7 us -> 66.3 us (0.979)
  Pallas kernels: 65.9 us -> 64.6 us
    pallas_call x1, Pallas kernels: 65.9 us -> 64.6 us  [local(): pl.pallas_call(kernel, out_shape=jax.ShapeDtypeStruct((8, 2 * COLS), BF16...]
where the time goes in v2:
time: 66.3 us; the launch traced here: 66.2 us
  Pallas kernels  64.6 us (97%)
  local copies, waits for them, and re-layouts  1.57 us (2%)
    pallas_call x1, Pallas kernels, local(): pl.pallas_call(kernel, out_shape=jax.ShapeDtypeStruct((8, 2 * COLS), BF16...  64.6 us
    unnamed x1, local copies, waits for them, and re-layouts  1.57 us

profile of v2, /device:TPU:1, one launch (start us, length us, event | category | flops | bytes accessed | tf_op | source)
XLA Modules:
  0.0 66.2 jit_solution(3443591014722615817)
XLA Ops:
  0.0 64.6 %attention_layer.1 = bf16[8,8192]{1,0:T(8,128)(2,1)} custom-call(bf16[128,512]{1,0:T(8,128)(2,1)} %q_ref.1, bf16[128,1024]{1,0:T(8,128)(2,1)} %k_ref.1, bf16[128,1024]{1,0:T(8,128)(2,1)} %v_ref.1, s32[2,96]{1,0:T(2,128)} %flags_ref.1, bf16[512,8192]{1,0:T(8,128)(2,1)} %w_ref.1), custom_call_target="tpu_custom_call" | custom-call | tf_op jit(solution)/shard_map/attention_layer/pallas_call | solution.py:413
  64.6 1.6 %copy.7 = bf16[8,8192]{1,0:T(8,128)(2,1)} copy(bf16[8,8192]{1,0:T(8,128)(2,1)} %attention_layer.1) | data formatting | bytes 262144

commit v3 on v2

--- a/solution.py
+++ b/solution.py
@@ -38,8 +38,12 @@
     def dev(rr, zz, xx, yy, cc):
         return {"ctx": rr * NZ + zz, "head": xx * 4 + yy * 2 + cc}
 
-    zp = dev(r, lax.rem(z + 1, NZ), x, yl, co)
-    zm = dev(r, lax.rem(z + NZ - 1, NZ), x, yl, co)
+    def ahead(way, d):
+        return lax.rem(z + NZ + (1 - 2 * way) * d, NZ)
+
+    def zdev(way, d):
+        return dev(r, ahead(way, d), x, yl, co)
+
     r_minus, r_plus, r_far = lax.rem(r - sg + NR, NR), lax.rem(r + sg + NR, NR), lax.rem(r + 2, NR)
     dev_a = dev(r_minus, z, x, 1 - yl, co)
     dev_b = dev(r_minus, z, x, yl, co)
@@ -79,7 +83,7 @@
     w_own.start()
 
     barrier = pltpu.get_barrier_semaphore()
-    peers = [zp, zm, dev_a, dev_b_src, dev_c, mate, ydev(0), ydev(1)]
+    peers = [zdev(way, d) for way in (0, 1) for d in (1, 2)] + [dev_a, dev_b_src, dev_c, mate, ydev(0), ydev(1)]
     peers += [xdev(d, cc) for d in (1, 2, 3) for cc in (0, 1)]
     for peer in peers:
         pl.semaphore_signal(barrier, inc=1, device_id=peer, device_id_type=MESH)
@@ -90,24 +94,50 @@
             src_ref=src, dst_ref=dst, send_sem=send_sem, recv_sem=recv_sem, device_id=peer, device_id_type=MESH
         )
 
-    def at_plus(d):
-        return lax.rem(z + NZ - d, NZ)
-
-    def at_minus(d):
-        return lax.rem(z + d, NZ)
-
-    def hop(way, d, j):
-        zi = at_plus(d) if way == 0 else at_minus(d)
-        return remote(kv.at[zi, j], kv.at[zi, j], tx.at[way, d, j], rx.at[way, d, j], zp if way == 0 else zm)
+    def hop(way, d, step, j):
+        zi = ahead(1 - way, d)
+        at = d + step - 1
+        return remote(kv.at[zi, j], kv.at[zi, j], tx.at[way, at, j], rx.at[way, at, j], zdev(way, step))
 
     def arrival(way, d, j):
-        zi = at_plus(d) if way == 0 else at_minus(d)
-        return remote(kv.at[zi, j], kv.at[zi, j], tx.at[way, d - 1, j], rx.at[way, d - 1, j], zp if way == 0 else zm)
+        zi = ahead(1 - way, d)
+        return remote(kv.at[zi, j], kv.at[zi, j], tx.at[way, d - 1, j], rx.at[way, d - 1, j], zdev(way, 1))
+
+    def comes(zz, way, d, j):
+        if j:
+            return row_of[j] < r
+        return ((way == 0) & (zz >= d)) | ((way == 1) & ((zz + d >= NZ) | (zz + d <= 4)))
+
+    def farthest(way, j):
+        return 6 - way if j < 2 else 5 + way
+
+    def goes(way, d, step, j):
+        return (d + step <= farthest(way, j)) & comes(ahead(way, step), way, d + step, j)
+
+    def send_on(way, d, j):
+        for step in (2, 1):
+
+            @pl.when(goes(way, d, step, j))
+            def _():
+                hop(way, d, step, j).start()
+
+    def clear(zi, carry):
+        @pl.when((zi > z) & (zi > 4))
+        def _():
+            kv[zi, 0] = jnp.zeros((HALF, 2 * HD), BF16)
+
+        for j in (1, 2, 3):
+
+            @pl.when(row_of[j] > r)
+            def _():
+                kv[zi, j] = jnp.zeros((HALF, 2 * HD), BF16)
+
+        return carry
 
     for copy in loads[:2]:
         copy.wait()
-    hop(0, 0, 0).start()
-    hop(1, 0, 0).start()
+    for way in (0, 1):
+        send_on(way, 0, 0)
     for copy in loads[2:4]:
         copy.wait()
     y_copies = [
@@ -115,8 +145,13 @@
         remote(kv.at[z, 0], kv.at[z, 2], ytx.at[1], yrx.at[1], dev_b),
         remote(oth, kv.at[z, 3], ytx.at[2], yrx.at[2], dev_c),
     ]
-    for copy in reversed(y_copies):
-        copy.start()
+    y_rows = (r_minus, r_minus, r_far)
+    for i in (2, 1, 0):
+
+        @pl.when(y_rows[i] > r)
+        def _():
+            y_copies[i].start()
+
     q_copy = remote(q_ref, qall.at[co], qsem.at[0], qsem.at[1], mate)
     q_copy.start()
     w_copy = remote(
@@ -138,30 +173,16 @@
             lax.broadcasted_iota(jnp.int32, (8, 2 * TOK), 0) == 0, FLOOR, 0.0
         )
 
-    def relay(way, d, j):
-        last = 6 if (j < 2) == (way == 0) else 5
-
-        def go():
-            arrival(way, d, j).wait_recv()
-
-        def on():
-            hop(way, d, j).start()
-
-        if isinstance(d, int):
-            if d <= last:
-                go()
-            if d < last:
-                on()
-        else:
-            pl.when(d <= last)(go)
-            pl.when(d < last)(on)
-
-    for way in (0, 1):
-        relay(way, 1, 0)
     for j in (1, 2, 3):
-        y_copies[j - 1].wait_recv()
-        hop(0, 0, j).start()
-        hop(1, 0, j).start()
+
+        @pl.when(row_of[j] < r)
+        def _():
+            y_copies[j - 1].wait_recv()
+
+        for way in (0, 1):
+            send_on(way, 0, j)
+
+    lax.fori_loop(0, NZ, clear, 0)
     flag_load.wait()
     def prepare(slot, zi):
         vt[slot] = kv[zi, :, :, HD:].reshape(4 * HALF, HD).T
@@ -198,31 +219,64 @@
         acc[g, HD + 1 : HD + 2] = total
         acc[g, :HD] = mixed
 
-    def relays(k, j):
-        for way in (0, 1):
-            relay(way, k + 1 if j == 0 else k, j)
-
+    def relay(way, d, j):
+        @pl.when((d <= farthest(way, j)) & comes(z, way, d, j))
+        def _():
+            arrival(way, d, j).wait_recv()
+
+        @pl.when(lax.rem(d, 2) == 0)
+        def _():
+            send_on(way, d, j)
+
+    def packed(*steps):
+        return sum((8 * way + d) * 16**i for i, (way, d) in enumerate(steps))
+
+    def by_place(first, second, other):
+        return jnp.where(z == 0, first, jnp.where(z == 1, second, other))
+
+    order_a = by_place(
+        packed((1, 2), (1, 4), (0, 2), (0, 4), (0, 5), (0, 6)),
+        packed((1, 2), (0, 1), (1, 4), (0, 4), (0, 5), (0, 6)),
+        packed((0, 2), (0, 1), (0, 4), (0, 3), (0, 5), (0, 6)),
+    )
+    order_b = by_place(
+        packed((1, 1), (1, 3), (0, 1), (1, 5), (0, 3), (1, 6)),
+        packed((1, 1), (1, 3), (0, 2), (0, 3), (1, 5), (1, 6)),
+        packed((1, 2), (1, 1), (1, 4), (1, 3), (1, 5), (1, 6)),
+    )
+
+    def unpack(code):
+        digit = lax.rem(code, 16)
+        return lax.div(digit, 8), lax.rem(digit, 8)
+
+    pair = (unpack(order_a), unpack(order_b))
     for j in range(4):
-        relays(1, j)
+        for way, d in pair:
+            relay(way, d, j)
         if j == 0:
             prepare(0, z)
         attend([(0, z)], j, diagonal=True)
 
-    def step(k, carry):
+    def step(i, carry):
+        code_a, code_b, held_a, held_b = carry
+        pair = (unpack(code_a), unpack(code_b))
         for j in range(4):
-            relays(k, j)
+            for way, d in pair:
+                relay(way, d, j)
             if j == 0:
-                prepare(0, at_plus(k - 1))
-                prepare(1, at_minus(k - 1))
-            attend([(0, at_plus(k - 1)), (1, at_minus(k - 1))], j)
-        return carry
-
-    lax.fori_loop(2, 7, step, 0)
+                prepare(0, held_a)
+                prepare(1, held_b)
+            attend([(0, held_a), (1, held_b)], j)
+        held = [ahead(1 - way, d) for way, d in pair]
+        return lax.div(code_a, 16), lax.div(code_b, 16), held[0], held[1]
+
+    held = [ahead(1 - way, d) for way, d in pair]
+    lax.fori_loop(1, 6, step, (lax.div(order_a, 16), lax.div(order_b, 16), held[0], held[1]))
 
     a_copies = [remote(acc.at[g], racc.at[g], atx.at[g], arx.at[g], mate) for g in range(4)]
-    prepare(0, at_minus(6))
+    prepare(0, ahead(0, 6))
     for g in range(4):
-        attend([(0, at_minus(6))], g)
+        attend([(0, ahead(0, 6))], g)
         a_copies[g].start()
 
     def place(xx, yy):
@@ -387,23 +441,27 @@
 
     lax.fori_loop(0, NC, stored, 0)
 
-    for copy in y_copies + [q_copy, w_copy] + a_copies:
+    for copy in [q_copy, w_copy] + a_copies:
         copy.wait_send()
-
-    def drain(d, carry):
+    for i in range(3):
+
+        @pl.when(y_rows[i] > r)
+        def _():
+            y_copies[i].wait_send()
+
+    def drain(i, carry):
+        d = 2 * i
         for j in range(4):
             for way in (0, 1):
-                if (j < 2) == (way == 0):
-                    hop(way, d, j).wait_send()
-                else:
-
-                    @pl.when(d < 5)
+                for step in (2, 1):
+
+                    @pl.when(goes(way, d, step, j))
                     def _():
-                        hop(way, d, j).wait_send()
+                        hop(way, d, step, j).wait_send()
 
         return carry
 
-    lax.fori_loop(0, 6, drain, 0)
+    lax.fori_loop(0, 3, drain, 0)
 
 
 def local(queries, key_rows, value_rows, block_flags, out_weight):

time: 66.3 us -> 65.8 us (level)
  the two profiles are of different devices: /device:TPU:1 before, /device:TPU:57 now
where the time goes in v3:
time: 65.8 us; the launch traced here: 65 us
  Pallas kernels  63.5 us (97%)
  local copies, waits for them, and re-layouts  1.57 us (2%)
    pallas_call x1, Pallas kernels, local(): pl.pallas_call(kernel, out_shape=jax.ShapeDtypeStruct((8, 2 * COLS), BF16...  63.5 us
    unnamed x1, local copies, waits for them, and re-layouts  1.57 us

profile of v3, /device:TPU:57, one launch (start us, length us, event | category | flops | bytes accessed | tf_op | source)
XLA Modules:
  0.0 65.0 jit_solution(10345508077375339076)
XLA Ops:
  0.0 63.5 %attention_layer.1 = bf16[8,8192]{1,0:T(8,128)(2,1)} custom-call(bf16[128,512]{1,0:T(8,128)(2,1)} %q_ref.1, bf16[128,1024]{1,0:T(8,128)(2,1)} %k_ref.1, bf16[128,1024]{1,0:T(8,128)(2,1)} %v_ref.1, s32[2,96]{1,0:T(2,128)} %flags_ref.1, bf16[512,8192]{1,0:T(8,128)(2,1)} %w_ref.1), custom_call_target="tpu_custom_call" | custom-call | tf_op jit(solution)/shard_map/attention_layer/pallas_call | solution.py:471
  63.5 1.6 %copy.7 = bf16[8,8192]{1,0:T(8,128)(2,1)} copy(bf16[8,8192]{1,0:T(8,128)(2,1)} %attention_layer.1) | data formatting | bytes 262144

commit v4 on v3

--- a/solution.py
+++ b/solution.py
@@ -27,7 +27,7 @@
 def kernel(
     q_ref, k_ref, v_ref, flags_ref, w_ref, out_ref,
     flags, obuf, kv, oth, qall, qt, vt, acc, racc, a2, wv, sbuf, own, r1, r1x, s2a, s2b, s2d, f0, f1, own2,
-    lsem, wsem, fsem, osem, ytx, yrx, tx, rx, qsem, wrem, atx, arx, t1, q1, t2, q2, t3, q3,
+    lsem, wsem, fsem, osem, ytx, yrx, tx, rx, utx, urx, qsem, wrem, atx, arx, t1, q1, t2, q2, t3, q3,
 ):
     c = lax.axis_index("ctx")
     h = lax.axis_index("head")
@@ -47,7 +47,6 @@
     r_minus, r_plus, r_far = lax.rem(r - sg + NR, NR), lax.rem(r + sg + NR, NR), lax.rem(r + 2, NR)
     dev_a = dev(r_minus, z, x, 1 - yl, co)
     dev_b = dev(r_minus, z, x, yl, co)
-    dev_b_src = dev(r_plus, z, x, yl, co)
     dev_c = dev(r_far, z, x, 1 - yl, co)
     mate = dev(r, z, x, yl, 1 - co)
 
@@ -83,7 +82,8 @@
     w_own.start()
 
     barrier = pltpu.get_barrier_semaphore()
-    peers = [zdev(way, d) for way in (0, 1) for d in (1, 2)] + [dev_a, dev_b_src, dev_c, mate, ydev(0), ydev(1)]
+    peers = [zdev(way, d) for way in (0, 1) for d in (1, 2)] + [dev_a, dev_c, mate, ydev(0), ydev(1)]
+    peers += [dev(rr, z, x, yl, co) for rr in (r_plus, r_minus, r_far)]
     peers += [xdev(d, cc) for d in (1, 2, 3) for cc in (0, 1)]
     for peer in peers:
         pl.semaphore_signal(barrier, inc=1, device_id=peer, device_id_type=MESH)
@@ -105,8 +105,12 @@
 
     def comes(zz, way, d, j):
         if j:
-            return row_of[j] < r
-        return ((way == 0) & (zz >= d)) | ((way == 1) & ((zz + d >= NZ) | (zz + d <= 4)))
+            late = ((way == 0) & (zz < d)) | ((way == 1) & (zz <= 5) & (zz + d >= 6))
+            return (row_of[j] < r) & jnp.logical_not(late)
+        source = zz + d
+        forth = (way == 0) & ((zz >= d) | (r < NR - 1))
+        back = (way == 1) & ((source >= NZ) | (source <= 4) | ((source >= 6) & (r < NR - 1)))
+        return forth | back
 
     def farthest(way, j):
         return 6 - way if j < 2 else 5 + way
@@ -122,7 +126,7 @@
                 hop(way, d, step, j).start()
 
     def clear(zi, carry):
-        @pl.when((zi > z) & (zi > 4))
+        @pl.when((zi > z) & ((zi == 5) | ((zi > 5) & (r == NR - 1))))
         def _():
             kv[zi, 0] = jnp.zeros((HALF, 2 * HD), BF16)
 
@@ -219,14 +223,37 @@
         acc[g, HD + 1 : HD + 2] = total
         acc[g, :HD] = mixed
 
+    def lift(zi, j):
+        rr = (r, r_plus, r_minus, r_far)[j]
+        return remote(kv.at[zi, 0], kv.at[zi, j], utx.at[zi - 6, j], urx.at[zi - 6, j], dev(rr, z, x, yl, co))
+
+    def lifted(zi, j):
+        return remote(kv.at[zi, j], kv.at[zi, j], utx.at[zi - 6, j], urx.at[zi - 6, j], dev(r_plus, z, x, yl, co))
+
     def relay(way, d, j):
-        @pl.when((d <= farthest(way, j)) & comes(z, way, d, j))
+        zi = ahead(1 - way, d)
+        here = (d <= farthest(way, j)) & comes(z, way, d, j)
+        late = (zi > 5) & (z <= 5) & (d <= farthest(way, j))
+
+        @pl.when(here)
         def _():
             arrival(way, d, j).wait_recv()
 
         @pl.when(lax.rem(d, 2) == 0)
         def _():
             send_on(way, d, j)
+
+        if j == 0:
+            for i in (1, 2, 3):
+
+                @pl.when(here & late & ((r, r_plus, r_minus, r_far)[i] > r))
+                def _():
+                    lift(zi, i).start()
+        else:
+
+            @pl.when(late & (row_of[j] < r))
+            def _():
+                lifted(zi, j).wait_recv()
 
     def packed(*steps):
         return sum((8 * way + d) * 16**i for i, (way, d) in enumerate(steps))
@@ -250,8 +277,12 @@
         return lax.div(digit, 8), lax.rem(digit, 8)
 
     pair = (unpack(order_a), unpack(order_b))
+    order_a, order_b = lax.div(order_a, 16), lax.div(order_b, 16)
+    after = (unpack(order_a), unpack(order_b))
+    for way, d in pair:
+        relay(way, d, 0)
     for j in range(4):
-        for way, d in pair:
+        for way, d in pair if j else after:
             relay(way, d, j)
         if j == 0:
             prepare(0, z)
@@ -260,18 +291,27 @@
     def step(i, carry):
         code_a, code_b, held_a, held_b = carry
         pair = (unpack(code_a), unpack(code_b))
+        code_a, code_b = lax.div(code_a, 16), lax.div(code_b, 16)
+        after = (unpack(code_a), unpack(code_b))
         for j in range(4):
-            for way, d in pair:
-                relay(way, d, j)
             if j == 0:
+
+                @pl.when(i < 5)
+                def _():
+                    for way, d in after:
+                        relay(way, d, 0)
+
                 prepare(0, held_a)
                 prepare(1, held_b)
+            else:
+                for way, d in pair:
+                    relay(way, d, j)
             attend([(0, held_a), (1, held_b)], j)
         held = [ahead(1 - way, d) for way, d in pair]
-        return lax.div(code_a, 16), lax.div(code_b, 16), held[0], held[1]
+        return code_a, code_b, held[0], held[1]
 
     held = [ahead(1 - way, d) for way, d in pair]
-    lax.fori_loop(1, 6, step, (lax.div(order_a, 16), lax.div(order_b, 16), held[0], held[1]))
+    lax.fori_loop(1, 6, step, (order_a, order_b, held[0], held[1]))
 
     a_copies = [remote(acc.at[g], racc.at[g], atx.at[g], arx.at[g], mate) for g in range(4)]
     prepare(0, ahead(0, 6))
@@ -462,6 +502,17 @@
         return carry
 
     lax.fori_loop(0, 3, drain, 0)
+
+    def passed(zi, carry):
+        for i in (1, 2, 3):
+
+            @pl.when((z <= 5) & ((r, r_plus, r_minus, r_far)[i] > r))
+            def _():
+                lift(zi, i).wait_send()
+
+        return carry
+
+    lax.fori_loop(6, NZ, passed, 0)
 
 
 def local(queries, key_rows, value_rows, block_flags, out_weight):
@@ -503,6 +554,8 @@
             dma((3,)),
             dma((2, 6, 4)),
             dma((2, 6, 4)),
+            dma((6, 4)),
+            dma((6, 4)),
             dma((2,)),
             dma((2,)),
             dma((4,)),

time: 65.8 us -> 67.9 us (1.032)
  Pallas kernels: 63.5 us -> 66.2 us
    pallas_call x1, Pallas kernels: 63.5 us -> 66.2 us  [local(): pl.pallas_call(kernel, out_shape=jax.ShapeDtypeStruct((8, 2 * COLS), BF16...]
where the time goes in v4:
time: 67.9 us; the launch traced here: 67.8 us
  Pallas kernels  66.2 us (97%)
  local copies, waits for them, and re-layouts  1.57 us (2%)
    pallas_call x1, Pallas kernels, local(): pl.pallas_call(kernel, out_shape=jax.ShapeDtypeStruct((8, 2 * COLS), BF16...  66.2 us
    unnamed x1, local copies, waits for them, and re-layouts  1.57 us

profile of v4, /device:TPU:57, one launch (start us, length us, event | category | flops | bytes accessed | tf_op | source)
XLA Modules:
  0.0 67.8 jit_solution(9600157885539103113)
XLA Ops:
  0.0 66.2 %attention_layer.1 = bf16[8,8192]{1,0:T(8,128)(2,1)} custom-call(bf16[128,512]{1,0:T(8,128)(2,1)} %q_ref.1, bf16[128,1024]{1,0:T(8,128)(2,1)} %k_ref.1, bf16[128,1024]{1,0:T(8,128)(2,1)} %v_ref.1, s32[2,96]{1,0:T(2,128)} %flags_ref.1, bf16[512,8192]{1,0:T(8,128)(2,1)} %w_ref.1), custom_call_target="tpu_custom_call" | custom-call | tf_op jit(solution)/shard_map/attention_layer/pallas_call | solution.py:522
  66.2 1.6 %copy.7 = bf16[8,8192]{1,0:T(8,128)(2,1)} copy(bf16[8,8192]{1,0:T(8,128)(2,1)} %attention_layer.1) | data formatting | bytes 262144

commit v5 on v3

--- a/solution.py
+++ b/solution.py
@@ -26,7 +26,7 @@
 
 def kernel(
     q_ref, k_ref, v_ref, flags_ref, w_ref, out_ref,
-    flags, obuf, kv, oth, qall, qt, vt, acc, racc, a2, wv, sbuf, own, r1, r1x, s2a, s2b, s2d, f0, f1, own2,
+    flags, obuf, kv, oth, qall, qt, vt, acc, racc, a2, wv, sbuf, own, r1, r1x, s2a, s2b, s2d, f0, f1, fm, own2,
     lsem, wsem, fsem, osem, ytx, yrx, tx, rx, qsem, wrem, atx, arx, t1, q1, t2, q2, t3, q3,
 ):
     c = lax.axis_index("ctx")
@@ -112,10 +112,12 @@
         return 6 - way if j < 2 else 5 + way
 
     def goes(way, d, step, j):
-        return (d + step <= farthest(way, j)) & comes(ahead(way, step), way, d + step, j)
+        if j:
+            return (step == 1) & (d + 1 <= farthest(way, j)) & comes(ahead(way, 1), way, d + 1, j)
+        return (lax.rem(d, 2) == 0) & (d + step <= farthest(way, j)) & comes(ahead(way, step), way, d + step, j)
 
     def send_on(way, d, j):
-        for step in (2, 1):
+        for step in (1,) if j else (2, 1):
 
             @pl.when(goes(way, d, step, j))
             def _():
@@ -224,9 +226,7 @@
         def _():
             arrival(way, d, j).wait_recv()
 
-        @pl.when(lax.rem(d, 2) == 0)
-        def _():
-            send_on(way, d, j)
+        send_on(way, d, j)
 
     def packed(*steps):
         return sum((8 * way + d) * 16**i for i, (way, d) in enumerate(steps))
@@ -235,14 +235,14 @@
         return jnp.where(z == 0, first, jnp.where(z == 1, second, other))
 
     order_a = by_place(
-        packed((1, 2), (1, 4), (0, 2), (0, 4), (0, 5), (0, 6)),
-        packed((1, 2), (0, 1), (1, 4), (0, 4), (0, 5), (0, 6)),
-        packed((0, 2), (0, 1), (0, 4), (0, 3), (0, 5), (0, 6)),
+        packed((1, 1), (1, 3), (0, 1), (0, 3), (0, 4), (0, 6)),
+        packed((1, 1), (1, 2), (0, 2), (0, 3), (0, 5), (0, 6)),
+        packed((0, 1), (0, 2), (0, 3), (0, 4), (0, 5), (0, 6)),
     )
     order_b = by_place(
-        packed((1, 1), (1, 3), (0, 1), (1, 5), (0, 3), (1, 6)),
-        packed((1, 1), (1, 3), (0, 2), (0, 3), (1, 5), (1, 6)),
-        packed((1, 2), (1, 1), (1, 4), (1, 3), (1, 5), (1, 6)),
+        packed((1, 2), (1, 4), (0, 2), (1, 5), (0, 5), (1, 6)),
+        packed((0, 1), (1, 3), (1, 4), (0, 4), (1, 5), (1, 6)),
+        packed((1, 1), (1, 2), (1, 3), (1, 4), (1, 5), (1, 6)),
     )
 
     def unpack(code):
@@ -279,12 +279,10 @@
         attend([(0, ahead(0, 6))], g)
         a_copies[g].start()
 
-    def place(xx, yy):
+    def places(xx, yy):
         dx = lax.rem(xx - x + NX + 3, NX)
         near = lax.rem(yy + yl, 2)
-        by_y = dx + 4 * (1 - near)
-        by_x = dx * 2 + near
-        return jnp.where(co == 0, by_y, by_x)
+        return dx + 4 * (1 - near), dx * 2 + near
 
     for g in range(4):
         a_copies[g].wait_recv()
@@ -299,140 +297,114 @@
             for xx in range(4):
                 for yy in range(2):
                     at = (xx * 2 + yy) * 16
-                    a2[place(xx, yy), :, cols] = tile[at : at + 16]
+                    for kind, place in enumerate(places(xx, yy)):
+                        a2[kind, place, :, cols] = tile[at : at + 16]
 
     w_own.wait()
     w_copy.wait_recv()
 
-    def send1y(n):
-        return remote(sbuf.at[n, pl.ds(0, 64)], r1.at[n], t1.at[0, n], q1.at[0, n], ydev(0))
-
-    def send1x(n, d):
-        return remote(
-            sbuf.at[n, pl.ds(32 * (d - 1), 32)], r1x.at[d - 1, n], t1.at[d - 1, n], q1.at[d - 1, n], xdev(d, 1)
-        )
-
-    def project(n, carry):
-        cols = pl.ds(pl.multiple_of(n * CW, CW), CW)
-        part = jnp.dot(
-            a2[...].reshape(TOK, 8 * HD), wv[:, :, cols].reshape(8 * HD, CW), preferred_element_type=F32
-        )
-        sbuf[n] = part[:96].astype(BF16)
-        own[n] = part[64:]
-
-        @pl.when(co == 0)
-        def _():
-            send1y(n).start()
-
-        @pl.when(co == 1)
-        def _():
-            for d in (2, 1, 3):
-                send1x(n, d).start()
-
-        return carry
-
-    lax.fori_loop(0, NC, project, 0)
-
-    def send2x(n, d, cc):
-        return remote(s2a.at[n, d - 1, cc], f0.at[d - 1, n], t2.at[d - 1, cc, n], q2.at[d - 1, n], xdev(d, cc))
-
-    def send2y(n, cc):
-        return remote(s2b.at[n, cc], f1.at[0, n], t2.at[0, cc, n], q2.at[3, n], ydev(cc))
+    def send1y(m):
+        return remote(sbuf.at[2 * m, pl.ds(0, 64)], r1.at[m], t1.at[3, m], q1.at[3, m], ydev(co))
+
+    def send1x(m, d):
+        rows = pl.ds(32 * (d - 1), 32)
+        return remote(sbuf.at[2 * m + 1, rows], r1x.at[d - 1, m], t1.at[d - 1, m], q1.at[d - 1, m], xdev(d, co))
+
+    def project(m, carry):
+        for kind in (1, 0):
+            n = 2 * m + kind
+            cols = pl.ds(pl.multiple_of(n * CW, CW), CW)
+            part = jnp.dot(
+                a2[kind].reshape(TOK, 8 * HD), wv[:, :, cols].reshape(8 * HD, CW), preferred_element_type=F32
+            )
+            sbuf[n] = part[:96].astype(BF16)
+            own[n] = part[64:]
+            if kind:
+                for d in (2, 1, 3):
+                    send1x(m, d).start()
+            else:
+                send1y(m).start()
+        return carry
+
+    lax.fori_loop(0, NC // 2, project, 0)
+
+    def send2x(m, d, cc, side):
+        return remote(s2a.at[m, d - 1, cc], f0.at[side, d - 1, m], t2.at[d - 1, cc, m], q2.at[side, d - 1, m], xdev(d, cc))
+
+    def send2y(m, cc, side):
+        return remote(s2b.at[m, cc], f1.at[side, m], t2.at[3, cc, m], q2.at[side, 3, m], ydev(cc))
+
+    def send3(n):
+        return remote(s2d.at[n, 1 - co], fm.at[n], t3.at[n], q3.at[n], mate)
+
+    def keep(n, total):
+        for cc in (0, 1):
+            own2[n, cc] = total[8 * cc : 8 * cc + 8]
+            s2d[n, cc] = total[8 * cc : 8 * cc + 8].astype(BF16)
+        send3(n).start()
+
+    def second(m, carry):
+        for d in (1, 2, 3):
+            send1x(m, d).wait_recv()
+        total = own[2 * m + 1, pl.ds(32, 32)]
+        for d in range(3):
+            total = total + r1x[d, m].astype(F32)
+        for cc in (0, 1):
+            s2b[m, cc] = total[16 + 8 * cc : 24 + 8 * cc].astype(BF16)
+            send2y(m, cc, co).start()
+        keep(2 * m + 1, total[:16])
+        send1y(m).wait_recv()
+        total = own[2 * m] + r1[m].astype(F32)
+        for d in (2, 1, 3):
+            for cc in (0, 1):
+                at = 16 * (d - 1) + 8 * cc
+                s2a[m, d - 1, cc] = total[at : at + 8].astype(BF16)
+                send2x(m, d, cc, co).start()
+        keep(2 * m, total[48:])
+        return carry
+
+    lax.fori_loop(0, NC // 2, second, 0)
 
     def put(side, n):
         at = pl.multiple_of(side * COLS + n * CW, CW)
         return pltpu.make_async_copy(obuf.at[side, n], out_ref.at[:, pl.ds(at, CW)], osem.at[side, n])
 
-    def send3a(n):
-        return remote(s2d.at[n], f0.at[3, n], t3.at[n], q3.at[n], mate)
-
-    def send3b(n):
-        return remote(s2d.at[n], f1.at[1, n], t3.at[n], q3.at[n], mate)
-
-    @pl.when(co == 0)
-    def _():
-        def second(n, carry):
-            send1y(n).wait_recv()
-            total = own[n] + r1[n].astype(F32)
-            for d in (2, 1, 3):
-                for cc in (0, 1):
-                    at = 16 * (d - 1) + 8 * cc
-                    s2a[n, d - 1, cc] = total[at : at + 8].astype(BF16)
-                    send2x(n, d, cc).start()
-            own2[n] = total[48:56]
-            s2d[n] = total[56:].astype(BF16)
-            send3a(n).start()
-            return carry
-
-        lax.fori_loop(0, NC, second, 0)
-
-        def last(n, carry):
+    def last(m, carry):
+        for side in (co, 1 - co):
+            mine = side is co
+            n = 2 * m + 1
+            if not mine:
+                send3(n).wait_recv()
+            send2y(m, 0, side).wait_recv()
+            total = own2[n, co] if mine else fm[n].astype(F32)
+            obuf[side, n] = (total + f1[side, m].astype(F32)).astype(BF16)
+            put(side, n).start()
+            n = 2 * m
+            if not mine:
+                send3(n).wait_recv()
+            total = own2[n, co] if mine else fm[n].astype(F32)
             for d in (1, 2, 3):
-                send2x(n, d, 0).wait_recv()
-            total = own2[n] + f0[0, n].astype(F32) + f0[1, n].astype(F32) + f0[2, n].astype(F32)
-            obuf[0, n] = total.astype(BF16)
-            put(0, n).start()
-            send2y(n, 0).wait_recv()
-            send3b(n).wait_recv()
-            total = f1[0, n].astype(F32) + f1[1, n].astype(F32)
-            obuf[1, n] = total.astype(BF16)
-            put(1, n).start()
-            return carry
-
-        lax.fori_loop(0, NC, last, 0)
-
-        def sent(n, carry):
-            send1y(n).wait_send()
-            for d in (1, 2, 3):
-                for cc in (0, 1):
-                    send2x(n, d, cc).wait_send()
-            send3a(n).wait_send()
-            return carry
-
-        lax.fori_loop(0, NC, sent, 0)
-
-    @pl.when(co == 1)
-    def _():
-        def second(n, carry):
-            for d in (1, 2, 3):
-                send1x(n, d).wait_recv()
-            total = own[n, pl.ds(32, 32)]
-            for d in range(3):
-                total = total + r1x[d, n].astype(F32)
+                send2x(m, d, 0, side).wait_recv()
+                total = total + f0[side, d - 1, m].astype(F32)
+            obuf[side, n] = total.astype(BF16)
+            put(side, n).start()
+        return carry
+
+    lax.fori_loop(0, NC // 2, last, 0)
+
+    def sent(m, carry):
+        for d in (1, 2, 3):
+            send1x(m, d).wait_send()
             for cc in (0, 1):
-                s2b[n, cc] = total[16 + 8 * cc : 24 + 8 * cc].astype(BF16)
-                send2y(n, cc).start()
-            s2d[n] = total[:8].astype(BF16)
-            send3b(n).start()
-            own2[n] = total[8:16]
-            return carry
-
-        lax.fori_loop(0, NC, second, 0)
-
-        def last(n, carry):
-            for d in (1, 2, 3):
-                send2x(n, d, 1).wait_recv()
-            send3a(n).wait_recv()
-            total = f0[3, n].astype(F32) + f0[0, n].astype(F32) + f0[1, n].astype(F32) + f0[2, n].astype(F32)
-            obuf[0, n] = total.astype(BF16)
-            put(0, n).start()
-            send2y(n, 1).wait_recv()
-            total = own2[n] + f1[0, n].astype(F32)
-            obuf[1, n] = total.astype(BF16)
-            put(1, n).start()
-            return carry
-
-        lax.fori_loop(0, NC, last, 0)
-
-        def sent(n, carry):
-            for d in (1, 2, 3):
-                send1x(n, d).wait_send()
-            for cc in (0, 1):
-                send2y(n, cc).wait_send()
-            send3b(n).wait_send()
-            return carry
-
-        lax.fori_loop(0, NC, sent, 0)
+                send2x(m, d, cc, co).wait_send()
+        send1y(m).wait_send()
+        for cc in (0, 1):
+            send2y(m, cc, co).wait_send()
+        for kind in (0, 1):
+            send3(2 * m + kind).wait_send()
+        return carry
+
+    lax.fori_loop(0, NC // 2, sent, 0)
 
     def stored(n, carry):
         for side in (0, 1):
@@ -449,11 +421,10 @@
         def _():
             y_copies[i].wait_send()
 
-    def drain(i, carry):
-        d = 2 * i
+    def drain(d, carry):
         for j in range(4):
             for way in (0, 1):
-                for step in (2, 1):
+                for step in (1,) if j else (2, 1):
 
                     @pl.when(goes(way, d, step, j))
                     def _():
@@ -461,7 +432,7 @@
 
         return carry
 
-    lax.fori_loop(0, 3, drain, 0)
+    lax.fori_loop(0, 6, drain, 0)
 
 
 def local(queries, key_rows, value_rows, block_flags, out_weight):
@@ -483,18 +454,19 @@
             vmem((2, HD, 4 * HALF), BF16),
             vmem((4, HD + 8, 2 * TOK), F32),
             vmem((4, HD + 8, 2 * TOK), F32),
-            vmem((8, 16, 8 * HD), BF16),
+            vmem((2, 8, 16, 8 * HD), BF16),
             vmem((2, 4 * HD, COLS), BF16),
             vmem((NC, 96, CW), BF16),
             vmem((NC, 64, CW), F32),
-            vmem((NC, 64, CW), BF16),
-            vmem((3, NC, 32, CW), BF16),
-            vmem((NC, 3, 2, 8, CW), BF16),
+            vmem((NC // 2, 64, CW), BF16),
+            vmem((3, NC // 2, 32, CW), BF16),
+            vmem((NC // 2, 3, 2, 8, CW), BF16),
+            vmem((NC // 2, 2, 8, CW), BF16),
             vmem((NC, 2, 8, CW), BF16),
+            vmem((2, 3, NC // 2, 8, CW), BF16),
+            vmem((2, NC // 2, 8, CW), BF16),
             vmem((NC, 8, CW), BF16),
-            vmem((4, NC, 8, CW), BF16),
-            vmem((2, NC, 8, CW), BF16),
-            vmem((NC, 8, CW), F32),
+            vmem((NC, 2, 8, CW), F32),
             dma((5,)),
             dma,
             dma,
@@ -507,10 +479,10 @@
             dma((2,)),
             dma((4,)),
             dma((4,)),
-            dma((3, NC)),
-            dma((3, NC)),
-            dma((3, 2, NC)),
-            dma((4, NC)),
+            dma((4, NC // 2)),
+            dma((4, NC // 2)),
+            dma((4, 2, NC // 2)),
+            dma((2, 4, NC // 2)),
             dma((NC,)),
             dma((NC,)),
         ],

time: 65.8 us -> 85.7 us (1.30)
  Pallas kernels: 63.5 us -> 84 us
    pallas_call x1, Pallas kernels: 63.5 us -> 84 us  [local(): pl.pallas_call(kernel, out_shape=jax.ShapeDtypeStruct((8, 2 * COLS), BF16...]
where the time goes in v5:
time: 85.7 us; the launch traced here: 85.6 us
  Pallas kernels  84 us (98%)
  local copies, waits for them, and re-layouts  1.57 us (2%)
    pallas_call x1, Pallas kernels, local(): pl.pallas_call(kernel, out_shape=jax.ShapeDtypeStruct((8, 2 * COLS), BF16...  84 us

profile of v5, /device:TPU:57, one launch (start us, length us, event | category | flops | bytes accessed | tf_op | source)
XLA Modules:
  0.0 85.6 jit_solution(4495902611696214782)
XLA Ops:
  0.0 84.0 %attention_layer.1 = bf16[8,8192]{1,0:T(8,128)(2,1)} custom-call(bf16[128,512]{1,0:T(8,128)(2,1)} %q_ref.1, bf16[128,1024]{1,0:T(8,128)(2,1)} %k_ref.1, bf16[128,1024]{1,0:T(8,128)(2,1)} %v_ref.1, s32[2,96]{1,0:T(2,128)} %flags_ref.1, bf16[512,8192]{1,0:T(8,128)(2,1)} %w_ref.1), custom_call_target="tpu_custom_call" | custom-call | tf_op jit(solution)/shard_map/attention_layer/pallas_call | solution.py:442
  84.0 1.6 %copy.7 = bf16[8,8192]{1,0:T(8,128)(2,1)} copy(bf16[8,8192]{1,0:T(8,128)(2,1)} %attention_layer.1) | data formatting | bytes 262144

commit v6 on v5

--- a/solution.py
+++ b/solution.py
@@ -38,12 +38,8 @@
     def dev(rr, zz, xx, yy, cc):
         return {"ctx": rr * NZ + zz, "head": xx * 4 + yy * 2 + cc}
 
-    def ahead(way, d):
-        return lax.rem(z + NZ + (1 - 2 * way) * d, NZ)
-
-    def zdev(way, d):
-        return dev(r, ahead(way, d), x, yl, co)
-
+    zp = dev(r, lax.rem(z + 1, NZ), x, yl, co)
+    zm = dev(r, lax.rem(z + NZ - 1, NZ), x, yl, co)
     r_minus, r_plus, r_far = lax.rem(r - sg + NR, NR), lax.rem(r + sg + NR, NR), lax.rem(r + 2, NR)
     dev_a = dev(r_minus, z, x, 1 - yl, co)
     dev_b = dev(r_minus, z, x, yl, co)
@@ -83,7 +79,7 @@
     w_own.start()
 
     barrier = pltpu.get_barrier_semaphore()
-    peers = [zdev(way, d) for way in (0, 1) for d in (1, 2)] + [dev_a, dev_b_src, dev_c, mate, ydev(0), ydev(1)]
+    peers = [zp, zm, dev_a, dev_b_src, dev_c, mate, ydev(0), ydev(1)]
     peers += [xdev(d, cc) for d in (1, 2, 3) for cc in (0, 1)]
     for peer in peers:
         pl.semaphore_signal(barrier, inc=1, device_id=peer, device_id_type=MESH)
@@ -94,34 +90,29 @@
             src_ref=src, dst_ref=dst, send_sem=send_sem, recv_sem=recv_sem, device_id=peer, device_id_type=MESH
         )
 
-    def hop(way, d, step, j):
-        zi = ahead(1 - way, d)
-        at = d + step - 1
-        return remote(kv.at[zi, j], kv.at[zi, j], tx.at[way, at, j], rx.at[way, at, j], zdev(way, step))
+    def at_plus(d):
+        return lax.rem(z + NZ - d, NZ)
+
+    def at_minus(d):
+        return lax.rem(z + d, NZ)
+
+    def hop(way, d, j):
+        zi = at_plus(d) if way == 0 else at_minus(d)
+        return remote(kv.at[zi, j], kv.at[zi, j], tx.at[way, d, j], rx.at[way, d, j], zp if way == 0 else zm)
 
     def arrival(way, d, j):
-        zi = ahead(1 - way, d)
-        return remote(kv.at[zi, j], kv.at[zi, j], tx.at[way, d - 1, j], rx.at[way, d - 1, j], zdev(way, 1))
+        zi = at_plus(d) if way == 0 else at_minus(d)
+        return remote(kv.at[zi, j], kv.at[zi, j], tx.at[way, d - 1, j], rx.at[way, d - 1, j], zp if way == 0 else zm)
 
     def comes(zz, way, d, j):
         if j:
             return row_of[j] < r
-        return ((way == 0) & (zz >= d)) | ((way == 1) & ((zz + d >= NZ) | (zz + d <= 4)))
-
-    def farthest(way, j):
-        return 6 - way if j < 2 else 5 + way
-
-    def goes(way, d, step, j):
-        if j:
-            return (step == 1) & (d + 1 <= farthest(way, j)) & comes(ahead(way, 1), way, d + 1, j)
-        return (lax.rem(d, 2) == 0) & (d + step <= farthest(way, j)) & comes(ahead(way, step), way, d + step, j)
-
-    def send_on(way, d, j):
-        for step in (1,) if j else (2, 1):
-
-            @pl.when(goes(way, d, step, j))
-            def _():
-                hop(way, d, step, j).start()
+        if way == 0:
+            return zz >= d
+        return (zz + d >= NZ) | (zz + d <= 4)
+
+    def goes(way, d, j):
+        return comes(lax.rem(z + 1, NZ) if way == 0 else lax.rem(z + NZ - 1, NZ), way, d + 1, j)
 
     def clear(zi, carry):
         @pl.when((zi > z) & (zi > 4))
@@ -139,7 +130,11 @@
     for copy in loads[:2]:
         copy.wait()
     for way in (0, 1):
-        send_on(way, 0, 0)
+
+        @pl.when(goes(way, 0, 0))
+        def _():
+            hop(way, 0, 0).start()
+
     for copy in loads[2:4]:
         copy.wait()
     y_copies = [
@@ -175,14 +170,26 @@
             lax.broadcasted_iota(jnp.int32, (8, 2 * TOK), 0) == 0, FLOOR, 0.0
         )
 
+    def relay(way, d, j):
+        last = 6 if (j < 2) == (way == 0) else 5
+
+        @pl.when((d <= last) & comes(z, way, d, j))
+        def _():
+            arrival(way, d, j).wait_recv()
+
+        @pl.when((d < last) & goes(way, d, j))
+        def _():
+            hop(way, d, j).start()
+
+    for way in (0, 1):
+        relay(way, 1, 0)
     for j in (1, 2, 3):
 
         @pl.when(row_of[j] < r)
         def _():
             y_copies[j - 1].wait_recv()
-
-        for way in (0, 1):
-            send_on(way, 0, j)
+            hop(0, 0, j).start()
+            hop(1, 0, j).start()
 
     lax.fori_loop(0, NZ, clear, 0)
     flag_load.wait()
@@ -221,62 +228,31 @@
         acc[g, HD + 1 : HD + 2] = total
         acc[g, :HD] = mixed
 
-    def relay(way, d, j):
-        @pl.when((d <= farthest(way, j)) & comes(z, way, d, j))
-        def _():
-            arrival(way, d, j).wait_recv()
-
-        send_on(way, d, j)
-
-    def packed(*steps):
-        return sum((8 * way + d) * 16**i for i, (way, d) in enumerate(steps))
-
-    def by_place(first, second, other):
-        return jnp.where(z == 0, first, jnp.where(z == 1, second, other))
-
-    order_a = by_place(
-        packed((1, 1), (1, 3), (0, 1), (0, 3), (0, 4), (0, 6)),
-        packed((1, 1), (1, 2), (0, 2), (0, 3), (0, 5), (0, 6)),
-        packed((0, 1), (0, 2), (0, 3), (0, 4), (0, 5), (0, 6)),
-    )
-    order_b = by_place(
-        packed((1, 2), (1, 4), (0, 2), (1, 5), (0, 5), (1, 6)),
-        packed((0, 1), (1, 3), (1, 4), (0, 4), (1, 5), (1, 6)),
-        packed((1, 1), (1, 2), (1, 3), (1, 4), (1, 5), (1, 6)),
-    )
-
-    def unpack(code):
-        digit = lax.rem(code, 16)
-        return lax.div(digit, 8), lax.rem(digit, 8)
-
-    pair = (unpack(order_a), unpack(order_b))
+    def relays(k, j):
+        for way in (0, 1):
+            relay(way, k + 1 if j == 0 else k, j)
+
     for j in range(4):
-        for way, d in pair:
-            relay(way, d, j)
+        relays(1, j)
         if j == 0:
             prepare(0, z)
         attend([(0, z)], j, diagonal=True)
 
-    def step(i, carry):
-        code_a, code_b, held_a, held_b = carry
-        pair = (unpack(code_a), unpack(code_b))
+    def step(k, carry):
         for j in range(4):
-            for way, d in pair:
-                relay(way, d, j)
+            relays(k, j)
             if j == 0:
-                prepare(0, held_a)
-                prepare(1, held_b)
-            attend([(0, held_a), (1, held_b)], j)
-        held = [ahead(1 - way, d) for way, d in pair]
-        return lax.div(code_a, 16), lax.div(code_b, 16), held[0], held[1]
-
-    held = [ahead(1 - way, d) for way, d in pair]
-    lax.fori_loop(1, 6, step, (lax.div(order_a, 16), lax.div(order_b, 16), held[0], held[1]))
+                prepare(0, at_plus(k - 1))
+                prepare(1, at_minus(k - 1))
+            attend([(0, at_plus(k - 1)), (1, at_minus(k - 1))], j)
+        return carry
+
+    lax.fori_loop(2, 7, step, 0)
 
     a_copies = [remote(acc.at[g], racc.at[g], atx.at[g], arx.at[g], mate) for g in range(4)]
-    prepare(0, ahead(0, 6))
+    prepare(0, at_minus(6))
     for g in range(4):
-        attend([(0, ahead(0, 6))], g)
+        attend([(0, at_minus(6))], g)
         a_copies[g].start()
 
     def places(xx, yy):
@@ -424,11 +400,11 @@
     def drain(d, carry):
         for j in range(4):
             for way in (0, 1):
-                for step in (1,) if j else (2, 1):
-
-                    @pl.when(goes(way, d, step, j))
-                    def _():
-                        hop(way, d, step, j).wait_send()
+                last = 6 if (j < 2) == (way == 0) else 5
+
+                @pl.when((d < last) & goes(way, d, j))
+                def _():
+                    hop(way, d, j).wait_send()
 
         return carry
 

time: 85.7 us -> 62.1 us (0.72)
  Pallas kernels: 84 us -> 60.4 us
    pallas_call x1, Pallas kernels: 84 us -> 60.4 us  [local(): pl.pallas_call(kernel, out_shape=jax.ShapeDtypeStruct((8, 2 * COLS), BF16...]
where the time goes in v6:
time: 62.1 us; the launch traced here: 62 us
  Pallas kernels  60.4 us (97%)
  local copies, waits for them, and re-layouts  1.57 us (3%)
    pallas_call x1, Pallas kernels, local(): pl.pallas_call(kernel, out_shape=jax.ShapeDtypeStruct((8, 2 * COLS), BF16...  60.4 us
    unnamed x1, local copies, waits for them, and re-layouts  1.57 us

profile of v6, /device:TPU:57, one launch (start us, length us, event | category | flops | bytes accessed | tf_op | source)
XLA Modules:
  0.0 62.0 jit_solution(10933447909376170004)
XLA Ops:
  0.0 60.4 %attention_layer.1 = bf16[8,8192]{1,0:T(8,128)(2,1)} custom-call(bf16[128,512]{1,0:T(8,128)(2,1)} %q_ref.1, bf16[128,1024]{1,0:T(8,128)(2,1)} %k_ref.1, bf16[128,1024]{1,0:T(8,128)(2,1)} %v_ref.1, s32[2,96]{1,0:T(2,128)} %flags_ref.1, bf16[512,8192]{1,0:T(8,128)(2,1)} %w_ref.1), custom_call_target="tpu_custom_call" | custom-call | tf_op jit(solution)/shard_map/attention_layer/pallas_call | solution.py:418
  60.4 1.6 %copy.7 = bf16[8,8192]{1,0:T(8,128)(2,1)} copy(bf16[8,8192]{1,0:T(8,128)(2,1)} %attention_layer.1) | data formatting | bytes 262144

commit v7 on v6

--- a/solution.py
+++ b/solution.py
@@ -111,8 +111,14 @@
             return zz >= d
         return (zz + d >= NZ) | (zz + d <= 4)
 
+    def farthest(way, j, zz):
+        if j == 1:
+            return jnp.where((zz > 5) == (way == 0), 6, 5)
+        return 6 if (j < 2) == (way == 0) else 5
+
     def goes(way, d, j):
-        return comes(lax.rem(z + 1, NZ) if way == 0 else lax.rem(z + NZ - 1, NZ), way, d + 1, j)
+        zz = lax.rem(z + 1, NZ) if way == 0 else lax.rem(z + NZ - 1, NZ)
+        return (d + 1 <= farthest(way, j, zz)) & comes(zz, way, d + 1, j)
 
     def clear(zi, carry):
         @pl.when((zi > z) & (zi > 4))
@@ -143,7 +149,7 @@
         remote(oth, kv.at[z, 3], ytx.at[2], yrx.at[2], dev_c),
     ]
     y_rows = (r_minus, r_minus, r_far)
-    for i in (2, 1, 0):
+    for i in (0, 1, 2):
 
         @pl.when(y_rows[i] > r)
         def _():
@@ -171,13 +177,11 @@
         )
 
     def relay(way, d, j):
-        last = 6 if (j < 2) == (way == 0) else 5
-
-        @pl.when((d <= last) & comes(z, way, d, j))
+        @pl.when((d <= farthest(way, j, z)) & comes(z, way, d, j))
         def _():
             arrival(way, d, j).wait_recv()
 
-        @pl.when((d < last) & goes(way, d, j))
+        @pl.when(goes(way, d, j))
         def _():
             hop(way, d, j).start()
 
@@ -400,9 +404,7 @@
     def drain(d, carry):
         for j in range(4):
             for way in (0, 1):
-                last = 6 if (j < 2) == (way == 0) else 5
-
-                @pl.when((d < last) & goes(way, d, j))
+                @pl.when(goes(way, d, j))
                 def _():
                     hop(way, d, j).wait_send()
 

time: 62.1 us -> 61.6 us (level)
  no operation moved by 1% of the time
where the time goes in v7:
time: 61.6 us; the launch traced here: 61.5 us
  Pallas kernels  59.9 us (97%)
  local copies, waits for them, and re-layouts  1.57 us (3%)
    pallas_call x1, Pallas kernels, local(): pl.pallas_call(kernel, out_shape=jax.ShapeDtypeStruct((8, 2 * COLS), BF16...  59.9 us
    unnamed x1, local copies, waits for them, and re-layouts  1.57 us

profile of v7, /device:TPU:57, one launch (start us, length us, event | category | flops | bytes accessed | tf_op | source)
XLA Modules:
  0.0 61.5 jit_solution(11583817751996375095)
XLA Ops:
  0.0 59.9 %attention_layer.1 = bf16[8,8192]{1,0:T(8,128)(2,1)} custom-call(bf16[128,512]{1,0:T(8,128)(2,1)} %q_ref.1, bf16[128,1024]{1,0:T(8,128)(2,1)} %k_ref.1, bf16[128,1024]{1,0:T(8,128)(2,1)} %v_ref.1, s32[2,96]{1,0:T(2,128)} %flags_ref.1, bf16[512,8192]{1,0:T(8,128)(2,1)} %w_ref.1), custom_call_target="tpu_custom_call" | custom-call | tf_op jit(solution)/shard_map/attention_layer/pallas_call | solution.py:420
  59.9 1.6 %copy.7 = bf16[8,8192]{1,0:T(8,128)(2,1)} copy(bf16[8,8192]{1,0:T(8,128)(2,1)} %attention_layer.1) | data formatting | bytes 262144

commit v8 on v7

--- a/solution.py
+++ b/solution.py
@@ -83,6 +83,25 @@
     peers += [xdev(d, cc) for d in (1, 2, 3) for cc in (0, 1)]
     for peer in peers:
         pl.semaphore_signal(barrier, inc=1, device_id=peer, device_id_type=MESH)
+    def clear(zi, carry):
+        @pl.when((zi > z) & (zi > 4))
+        def _():
+            kv[zi, 0] = jnp.zeros((HALF, 2 * HD), BF16)
+
+        for j in (1, 2, 3):
+
+            @pl.when(row_of[j] > r)
+            def _():
+                kv[zi, j] = jnp.zeros((HALF, 2 * HD), BF16)
+
+        return carry
+
+    lax.fori_loop(0, NZ, clear, 0)
+    for g in range(4):
+        acc[g, :HD] = jnp.zeros((HD, 2 * TOK), F32)
+        acc[g, HD : HD + 8] = jnp.where(
+            lax.broadcasted_iota(jnp.int32, (8, 2 * TOK), 0) == 0, FLOOR, 0.0
+        )
     pl.semaphore_wait(barrier, len(peers))
 
     def remote(src, dst, send_sem, recv_sem, peer):
@@ -119,19 +138,6 @@
     def goes(way, d, j):
         zz = lax.rem(z + 1, NZ) if way == 0 else lax.rem(z + NZ - 1, NZ)
         return (d + 1 <= farthest(way, j, zz)) & comes(zz, way, d + 1, j)
-
-    def clear(zi, carry):
-        @pl.when((zi > z) & (zi > 4))
-        def _():
-            kv[zi, 0] = jnp.zeros((HALF, 2 * HD), BF16)
-
-        for j in (1, 2, 3):
-
-            @pl.when(row_of[j] > r)
-            def _():
-                kv[zi, j] = jnp.zeros((HALF, 2 * HD), BF16)
-
-        return carry
 
     for copy in loads[:2]:
         copy.wait()
@@ -170,11 +176,6 @@
     for i in range(8):
         side = slice((i % 2) * TOK, (i % 2 + 1) * TOK)
         qt[i // 2, :, side] = qall[i // 4, :, (i % 4) * HD : (i % 4 + 1) * HD].T
-    for g in range(4):
-        acc[g, :HD] = jnp.zeros((HD, 2 * TOK), F32)
-        acc[g, HD : HD + 8] = jnp.where(
-            lax.broadcasted_iota(jnp.int32, (8, 2 * TOK), 0) == 0, FLOOR, 0.0
-        )
 
     def relay(way, d, j):
         @pl.when((d <= farthest(way, j, z)) & comes(z, way, d, j))
@@ -195,7 +196,6 @@
             hop(0, 0, j).start()
             hop(1, 0, j).start()
 
-    lax.fori_loop(0, NZ, clear, 0)
     flag_load.wait()
     def prepare(slot, zi):
         vt[slot] = kv[zi, :, :, HD:].reshape(4 * HALF, HD).T

time: 61.6 us -> 61.6 us (level)
  no operation moved by 1% of the time
where the time goes in v8:
time: 61.6 us; the launch traced here: 61.5 us
  Pallas kernels  59.9 us (97%)
  local copies, waits for them, and re-layouts  1.57 us (3%)
    pallas_call x1, Pallas kernels, local(): pl.pallas_call(kernel, out_shape=jax.ShapeDtypeStruct((8, 2 * COLS), BF16...  59.9 us
    unnamed x1, local copies, waits for them, and re-layouts  1.57 us

profile of v8, /device:TPU:57, one launch (start us, length us, event | category | flops | bytes accessed | tf_op | source)
XLA Modules:
  0.0 61.5 jit_solution(7031994036168747025)
XLA Ops:
  0.0 59.9 %attention_layer.1 = bf16[8,8192]{1,0:T(8,128)(2,1)} custom-call(bf16[128,512]{1,0:T(8,128)(2,1)} %q_ref.1, bf16[128,1024]{1,0:T(8,128)(2,1)} %k_ref.1, bf16[128,1024]{1,0:T(8,128)(2,1)} %v_ref.1, s32[2,96]{1,0:T(2,128)} %flags_ref.1, bf16[512,8192]{1,0:T(8,128)(2,1)} %w_ref.1), custom_call_target="tpu_custom_call" | custom-call | tf_op jit(solution)/shard_map/attention_layer/pallas_call | solution.py:420
  59.9 1.6 %copy.7 = bf16[8,8192]{1,0:T(8,128)(2,1)} copy(bf16[8,8192]{1,0:T(8,128)(2,1)} %attention_layer.1) | data formatting | bytes 262144
